TPU v7x, 32 devices: a whole 2x2x4 slice. The times are simulated.
32 devices in a mesh: rep: 4 (over x, core), col: 8 (over z, y).
Axes of the slice: x: 2, y: 2, z: 4, core: 2. Of those that a mesh axis runs over, the one named last changes fastest.
Arguments:
- tokens_learn: bfloat16 [5120, 1024], P(None, 'rep'), may hold values from -6 to 6
- cotangent: bfloat16 [1024, 27648], P('rep', 'col'), may hold values from -6 to 6
- sample_ids: int32 [4, 256], P('rep'), may hold values from 0 to 7, never falling along the last dimension, each value on 1 to 64 neighbouring positions
- advantage: float32 [4, 8], P('rep'), may hold values from -2 to 2
- up_weight: bfloat16 [5120, 27648], P('rep', 'col'), may hold values from -0.078125 to 0.078125
- first_moment: float32 [5120, 27648], P('rep', 'col'), may hold values from -3 to 3
- second_moment: float32 [5120, 27648], P('rep', 'col'), may hold values from 0.05 to 1
- rollout_rows: bfloat16 [512, 5120], P('rep', 'col'), may hold values from -6 to 6
- down_proj: bfloat16 [5120, 27648], P(None, 'col'), may hold values from -0.0390625 to 0.0390625
- live_lengths: int32 [4, 4], P('rep'), may hold values from 1 to 32, 96 in all within a row
Outputs:
- new_weight: bfloat16 [5120, 27648], P('rep', 'col')
- new_first: float32 [5120, 27648], P('rep', 'col')
- new_second: float32 [5120, 27648], P('rep', 'col')
- rollout_out: bfloat16 [5120, 512], P('col', 'rep')
Inputs may be any that keep to these rules, and one draw needn't show every extreme that they name: `sample_ids`: each lane's sample ids never fall along the lane, and each of the 8 samples has 1 to 64 tokens of that lane. `live_lengths`: the 4 lengths of a replica sum to 96, and one of them is 32.
All inputs are finite; a program needn't handle non-finite values.
Results may differ from a plain program's by a relative error of at most 0.019.
Values may be sent and summed in bfloat16 or wider, within the bound.
No kernel may reach another device: no remote copies, remote signals or barrier semaphores. Data moves between devices by JAX's collectives and lax.ppermute only.
A program may use at most 256 MiB of HBM per device.

v0:
```python
import functools
import math

import jax
import jax.numpy as jnp
from jax import lax
from jax.experimental import pallas as pl
from jax.experimental.pallas import tpu as pltpu
from jax.sharding import PartitionSpec as P


SEQS = 4
LIVE = 96


VMEM_ADAM = 40 * 1024 * 1024
VMEM_DOWN = 32 * 1024 * 1024

first_decay = 0.9
second_decay = 0.95
learn_rate = 0.003
decay_weight = 0.1
adam_epsilon = 1e-08
first_bias = 1.0 - math.exp(100.0 * math.log(0.9))
second_bias = 1.0 - math.exp(100.0 * math.log(0.95))
second_root = math.sqrt(second_bias)


def token_scales(sample_ids, advantage):
    members = (sample_ids[..., :, None] == jnp.arange(advantage.shape[-1], dtype=jnp.int32)).astype(
        jnp.float32
    )
    counts = jnp.sum(members, axis=-2)
    ratios = advantage / counts
    return jnp.sum(members * ratios[..., None, :], axis=-1)


def live_picks(lengths, rows_each):
    slot_len = rows_each // SEQS
    slots = jnp.arange(SEQS, dtype=jnp.int32)
    before = jnp.sum(jnp.where(slots[None, :] < slots[:, None], lengths[None, :], 0), axis=1)
    rows = jnp.arange(rows_each, dtype=jnp.int32)
    which, within = rows // slot_len, rows % slot_len
    slot = (which[:, None] == jnp.arange(SEQS, dtype=jnp.int32)[None, :]).astype(jnp.int32)
    start = jnp.sum(slot * before[None, :], axis=1)
    limit = jnp.sum(slot * lengths[None, :], axis=1)
    place = jnp.where(within < limit, start + within, -1)
    return (jnp.arange(LIVE, dtype=jnp.int32)[:, None] == place[None, :]).astype(jnp.bfloat16)


def adam_kernel(lanes, chained, previous, own, *refs):
    refs = list(refs)
    token_refs, scaled_refs = refs[:lanes], refs[lanes : 2 * lanes]
    w_ref, m_ref, v_ref, x_ref = refs[2 * lanes : 2 * lanes + 4]
    refs = refs[2 * lanes + 4 :]
    past_w = refs[0] if chained else None
    new_w, new_m, new_v, *products = refs[3 if chained else 0 :]
    scaled = jnp.concatenate([ref[...] for ref in scaled_refs], axis=0)
    high = new_w.shape[0]
    part = 256 if high % 256 == 0 else high
    for top in range(0, high, part):
        span = slice(top, top + part)
        tokens = jnp.concatenate([ref[span, :] for ref in token_refs], axis=1)
        gradient = jnp.dot(tokens, scaled, preferred_element_type=jnp.float32)
        first = first_decay * m_ref[span, :] + (1.0 - first_decay) * gradient
        second = second_decay * v_ref[span, :] + ((1.0 - second_decay) * gradient) * gradient
        new_m[span, :] = first
        new_v[span, :] = second
        size = jnp.sqrt(second) + adam_epsilon * second_root
        wide = w_ref[span, :].astype(jnp.float32)
        step = (learn_rate * second_root / first_bias) * first / size
        new_w[span, :] = ((1.0 - learn_rate * decay_weight) * wide - step).astype(new_w.dtype)
    for k, source in enumerate(([past_w] if previous else []) + ([new_w] if own else [])):
        keep_ref, send_ref = products
        half = keep_ref.shape[1]
        value = jnp.dot(x_ref[...], source[...], preferred_element_type=jnp.float32)
        keep_ref[k] = value[:half].astype(keep_ref.dtype)
        send_ref[k] = value[half:].astype(send_ref.dtype)


def adam_chunk(tokens, scaled, weight, first, second, rows, chain, start, tile, previous, own):
    lanes, width, high = len(tokens), scaled[0].shape[1], weight.shape[0]
    skip = start // tile
    block = pl.BlockSpec((high, tile), lambda i: (0, i + skip))
    whole = lambda a: pl.BlockSpec(a.shape, lambda i: (0, 0))
    x_arg = rows if rows is not None else jnp.zeros((16, 128), jnp.bfloat16)
    args = [*tokens, *scaled, weight, first, second, x_arg]
    specs = [whole(t) for t in tokens]
    specs += [pl.BlockSpec((s.shape[0], tile), lambda i: (0, i)) for s in scaled]
    specs += [block, block, block, whole(x_arg)]
    alias = {}
    for k, c in enumerate(chain or ()):
        alias[len(args)] = k
        args.append(c)
        if k == 0 and previous:
            back = width // tile
            specs.append(pl.BlockSpec((high, tile), lambda i: (0, i + skip - back)))
        else:
            specs.append(pl.BlockSpec(memory_space=pl.ANY))
    outs = [jax.ShapeDtypeStruct(a.shape, a.dtype) for a in (weight, first, second)]
    out_specs = [block, block, block]
    groups = int(previous) + int(own)
    if groups:
        half = rows.shape[0] // 2
        outs += [jax.ShapeDtypeStruct((groups, half, width), jnp.bfloat16)] * 2
        out_specs += [pl.BlockSpec((groups, half, tile), lambda i: (0, 0, i))] * 2
    return pl.pallas_call(
        functools.partial(adam_kernel, lanes, bool(chain), previous, own),
        out_shape=outs,
        grid=(pl.cdiv(width, tile),),
        in_specs=specs,
        out_specs=out_specs,
        input_output_aliases=alias,
        cost_estimate=pl.CostEstimate(
            flops=2 * high * width * (lanes * tokens[0].shape[1] + groups * LIVE * 4),
            bytes_accessed=high * width * 20,
            transcendentals=high * width,
        ),
        compiler_params=pltpu.CompilerParams(vmem_limit_bytes=VMEM_ADAM),
    )(*args)


def down_kernel(groups, last, *refs):
    where_ref, *refs = refs
    own_refs, other_refs = refs[:groups], refs[groups : 2 * groups]
    first_ref, second_ref = refs[2 * groups : 2 * groups + 2]
    weights = jnp.concatenate([first_ref[...], second_ref[...]], axis=0)
    live = own_refs[0].shape[0]
    total = None
    for k in range(groups):
        width = own_refs[k].shape[1]
        act = jnp.concatenate([own_refs[k][...], other_refs[k][...]], axis=0)
        term = lax.dot_general(
            act,
            weights[:, k * width : (k + 1) * width],
            (((1,), (1,)), ((), ())),
            preferred_element_type=jnp.float32,
        )
        total = term if total is None else total + term
    if last:
        past_ref, own_out, other_out = refs[2 * groups + 2 :]
        total = total + past_ref[...]
        own_out[...] = total[:live].astype(own_out.dtype)
        other_out[...] = total[live:].astype(other_out.dtype)
    else:
        refs[-1][...] = total


def down_part(down_proj, own, other, where, start, past):
    cols = 8
    groups, (live, width) = len(own), own[0].shape
    unit = down_proj.shape[0] // cols // 2
    span = groups * width
    bits = lambda i: (i // 2) + 2 * (i % 2)

    def weight_spec(top):
        if start % span == 0:
            return pl.BlockSpec(
                (unit, span), lambda i, w: ((w[0] ^ (bits(i) + top)) * 2 + w[1], start // span)
            )
        return pl.BlockSpec(
            (pl.Element(unit), pl.Element(span)),
            lambda i, w: (((w[0] ^ (bits(i) + top)) * 2 + w[1]) * unit, start),
        )

    whole = lambda a: pl.BlockSpec(a.shape, lambda i, w: (0, 0))
    args = [*own, *other, down_proj, down_proj]
    specs = [whole(a) for a in (*own, *other)] + [weight_spec(0), weight_spec(4)]
    if past is None:
        outs = jax.ShapeDtypeStruct((2 * live, 8 * unit), jnp.float32)
        out_specs = pl.BlockSpec((2 * live, 2 * unit), lambda i, w: (0, i))
    else:
        args.append(past)
        specs.append(pl.BlockSpec((2 * live, 2 * unit), lambda i, w: (0, i)))
        outs = [jax.ShapeDtypeStruct((live, 8 * unit), jnp.bfloat16)] * 2
        out_specs = [
            pl.BlockSpec((live, 2 * unit), lambda i, w: (0, i)),
            pl.BlockSpec((live, 2 * unit), lambda i, w: (0, bits(i))),
        ]
    return pl.pallas_call(
        functools.partial(down_kernel, groups, past is not None),
        out_shape=outs,
        grid_spec=pltpu.PrefetchScalarGridSpec(
            num_scalar_prefetch=1, grid=(4,), in_specs=specs, out_specs=out_specs
        ),
        cost_estimate=pl.CostEstimate(
            flops=4 * live * 8 * unit * span, bytes_accessed=8 * unit * span * 2, transcendentals=0
        ),
        compiler_params=pltpu.CompilerParams(vmem_limit_bytes=VMEM_DOWN),
    )(where, *args)


def xor_pairs(count, bit):
    return [(i, i ^ bit) for i in range(count)]


def column_chunks(columns):
    tile = 256
    if columns % 128 or columns < 4 * tile:
        return [(0, columns)], columns
    tiles = -(-columns // tile)
    first = -(-tiles * 5 // 14)
    edges = [0, first * tile, 2 * first * tile, columns]
    return [(a, b - a) for a, b in zip(edges, edges[1:])], tile


def inner(
    reps,
    cols,
    tokens_learn,
    cotangent,
    sample_ids,
    advantage,
    up_weight,
    first_moment,
    second_moment,
    rollout_rows,
    down_proj,
    live_lengths,
):
    rep, col = lax.axis_index("rep"), lax.axis_index("col")
    swap_rep = lambda a, bit: lax.ppermute(a, "rep", xor_pairs(reps, bit))
    swap_col = lambda a, bit: lax.ppermute(a, "col", xor_pairs(cols, bit))
    bits = [1 << k for k in reversed(range(reps.bit_length() - 1))]
    f32, bf16 = jnp.float32, jnp.bfloat16

    features, depth = tokens_learn.shape
    high = features // reps
    quarter = high // 4
    blocks = tokens_learn.reshape(reps, 4, quarter, depth)
    part = col & 3

    def piece(j, which):
        return lax.dynamic_slice(blocks, (rep ^ j, which, 0, 0), (1, 1, quarter, depth))[0, 0]

    far = range(2, reps)
    near = lax.dynamic_index_in_dim(blocks, rep ^ 1, 0, keepdims=False).reshape(high, depth)
    pieces = [piece(j, part) for j in far]
    pieces, near, sample_ids, live_lengths = lax.optimization_barrier(
        (pieces, near, sample_ids, live_lengths)
    )
    straight = {}
    for j in far:
        straight[j] = swap_rep(pieces[j - 2], j)
    near = swap_rep(near, 1)

    token_scale = token_scales(sample_ids, advantage)[0]
    columns = cotangent.shape[1]
    chunks, tile = column_chunks(columns)
    scaled = []
    for start, width in chunks:
        own = lax.slice_in_dim(cotangent, start, start + width, axis=1)
        lanes = {0: (token_scale[:, None] * own.astype(f32)).astype(bf16)}
        for bit in bits:
            for j, value in list(lanes.items()):
                lanes[j | bit] = swap_rep(value, bit)
        scaled.append([lanes[j] for j in range(reps)])

    tokens = [lax.dynamic_index_in_dim(blocks, rep, 0, keepdims=False).reshape(high, depth), near]
    for j in far:
        second = swap_col(straight[j], 2)
        third = swap_col(straight[j], 1)
        fourth = swap_col(second, 1)
        got = [straight[j], third, second, fourth]
        tokens.append(jnp.concatenate([lax.select_n(part ^ i, *got) for i in range(4)], axis=0))

    picks = live_picks(live_lengths[0], rollout_rows.shape[0])
    compact = jnp.dot(picks, rollout_rows, preferred_element_type=f32).astype(bf16)
    per = cols // reps
    slabs = [compact]
    for i in range(1, reps):
        slabs.append(swap_col(compact, i * per))
    turn = (col // per) ^ rep
    order = [0]
    for bit in bits:
        order += [j | bit for j in order]
    rows = []
    for j in order:
        slab = lax.select_n(turn ^ j, *slabs)
        rows.append(slab if j == 0 else swap_rep(slab, j))
    rows = jnp.concatenate(rows, axis=0)
    for k in range(per.bit_length() - 1):
        other = swap_col(rows, 1 << k)
        upper = (col >> k) & 1
        rows = jnp.concatenate(
            [jnp.where(upper == 0, rows, other), jnp.where(upper == 0, other, rows)], axis=1
        )

    def reduced(keep, send):
        got = swap_rep(send, 1)
        value = keep.astype(f32) + got.astype(f32)
        for bit in bits[-2::-1]:
            half = value.shape[1] // 2
            got = swap_rep(value[:, half:].astype(bf16), bit)
            value = value[:, :half] + got.astype(f32)
        return jax.nn.silu(value).astype(bf16)

    chain, acts = None, []
    unit = features // cols
    paired = cols == 8 and unit % 128 == 0 and unit % 32 == 0 and len(chunks) == 3
    for index, ((start, width), lanes) in enumerate(zip(chunks, scaled)):
        only = len(chunks) == 1
        previous, own = (not only and index == 1), (only or index > 0)
        *out, = adam_chunk(
            tokens, lanes, up_weight, first_moment, second_moment,
            rows if own or previous else None, chain, start, tile, previous, own,
        )
        chain = out[:3]
        if own:
            act = reduced(*out[3:])
            acts += [act[k] for k in range(act.shape[0])]

    if paired:
        where = jnp.stack([col, rep & 1]).astype(jnp.int32)
        pair = swap_rep(jnp.stack(acts[:2]), 1)
        past = down_part(down_proj, acts[:2], [pair[0], pair[1]], where, 0, None)
        pair = swap_rep(acts[2], 1)
        own, other = down_part(down_proj, acts[2:], [pair], where, chunks[2][0], past)

        def stage(value, bit):
            half = value.shape[1] // 2
            got = swap_col(value[:, half:], bit)
            return (value[:, :half].astype(f32) + got.astype(f32)).astype(bf16)

        for one, two in ((1, 2), (2, 1), (4, 4)):
            own, other = stage(own, one), stage(other, two)
        other = swap_rep(other, 1)
        lower = (rep & 1) == 0
        held = jnp.concatenate([jnp.where(lower, own, other), jnp.where(lower, other, own)], axis=1)
        rollout_out = lax.dot_general(
            held, picks, (((0,), (0,)), ((), ())), preferred_element_type=f32
        ).astype(bf16)
        return (*chain, rollout_out)

    total = None
    for (start, width), act in zip(chunks, acts):
        term = lax.dot_general(
            lax.slice_in_dim(down_proj, start, start + width, axis=1),
            act,
            (((1,), (1,)), ((), ())),
            preferred_element_type=f32,
        )
        total = term if total is None else total + term
    held = total.reshape(cols, unit, LIVE)
    bit = cols // 2
    while bit:
        pairs = held.reshape(2, bit, unit, LIVE)
        upper = (col // bit) & 1
        mine = lax.dynamic_index_in_dim(pairs, upper, 0, keepdims=False)
        theirs = lax.dynamic_index_in_dim(pairs, 1 - upper, 0, keepdims=False)
        held = mine + swap_col(theirs.astype(bf16), bit).astype(f32)
        bit //= 2
    rollout_out = jnp.dot(held[0].astype(bf16), picks, preferred_element_type=f32).astype(bf16)
    return (*chain, rollout_out)


def body(reps, cols, *args):
    return inner(reps, cols, *args)


def solution(mesh):
    placed = (
        P(None, "rep"),
        P("rep", "col"),
        P("rep", None),
        P("rep", None),
        P("rep", "col"),
        P("rep", "col"),
        P("rep", "col"),
        P("rep", "col"),
        P(None, "col"),
        P("rep", None),
    )
    return jax.shard_map(
        functools.partial(body, mesh.shape["rep"], mesh.shape["col"]),
        mesh=mesh,
        in_specs=placed,
        out_specs=(P("rep", "col"), P("rep", "col"), P("rep", "col"), P("col", "rep")),
        check_vma=False,
    )
```

profile of v0, /device:TPU:0, one launch (start us, length us, event | category | flops | bytes accessed | tf_op | source)
XLA Modules:
  0.0 174.1 jit_solution(6921799681044797544)
XLA Ops:
  0.7 1.4 constant_dynamic-slice_fusion
  2.1 1.7 dynamic-slice_bitcast_fusion
  4.2 3.1 %collective-permute-start.12 = (bf16[96,640]{1,0:T(8,128)(2,1)S(1)}, bf16[96,640]{1,0:T(8,128)(2,1)S(1)}, u32[]{:S(2)}, u32[]{:S(2)}) collective-permute-start(bf16[96,640]{1,0:T(8,128)(2,1)S(1)} %convolution_convert_fusion.1), channel_id=1, source_target_pairs={{0,2},{1,3},{2,0},{3,1},{4,6},{5,7},{6,4},{7,5},{8,10},{9,11},{10,... | collective-permute-start | bytes 368648 | tf_op jit(solution)/shard_map/ppermute | solution.py:223
  7.4 2.6 %collective-permute-start.13 = (bf16[96,640]{1,0:T(8,128)(2,1)S(1)}, bf16[96,640]{1,0:T(8,128)(2,1)S(1)}, u32[]{:S(2)}, u32[]{:S(2)}) collective-permute-start(bf16[96,640]{1,0:T(8,128)(2,1)S(1)} %convolution_convert_fusion.1), channel_id=1, source_target_pairs={{0,4},{1,5},{2,6},{3,7},{4,0},{5,1},{6,2},{7,3},{8,12},{9,13},{10,... | collective-permute-start | bytes 368648 | tf_op jit(solution)/shard_map/ppermute | solution.py:223
  10.3 1.3 collective-permute-start.1
  12.1 7.6 %collective-permute-done.13 = bf16[96,640]{1,0:T(8,128)(2,1)S(1)} collective-permute-done((bf16[96,640]{1,0:T(8,128)(2,1)S(1)}, bf16[96,640]{1,0:T(8,128)(2,1)S(1)}, u32[]{:S(2)}, u32[]{:S(2)}) %collective-permute-start.13) | collective-permute-done | bytes 122912 | tf_op jit(solution)/shard_map/ppermute | solution.py:223
  19.7 0.7 select_select_fusion.11
  20.4 1.5 collective-permute-start.15
  21.9 1.9 %collective-permute-start.7 = (bf16[320,256]{1,0:T(8,128)(2,1)S(1)}, bf16[320,256]{1,0:T(8,128)(2,1)}, u32[]{:S(2)}, u32[]{:S(2)}) collective-permute-start(bf16[320,256]{1,0:T(8,128)(2,1)S(1)} %collective-permute-done.5), channel_id=1, source_target_pairs={{0,2},{1,3},{2,0},{3,1},{4,6},{5,7},{6,4},{7,5},{8,10},{9,11},{10,... | collective-permute-start | bytes 491528 | tf_op jit(solution)/shard_map/ppermute | solution.py:223
  23.8 1.6 multiply_convert_fusion
  25.4 0.6 collective-permute-start.23
  26.0 1.0 collective-permute-start.17
  27.0 1.5 collective-permute-start.6
  28.8 1.5 collective-permute-start.8
  30.3 1.9 %multiply_convert_fusion.3.refs_4_ = bf16[256,896]{1,0:T(8,128)(2,1)} fusion(bf16[256,3456]{1,0:T(8,128)(2,1)} %param.11, f32[256]{0:T(256)S(1)} %select_reduce_fusion), kind=kLoop, calls=%fused_computation.9 | loop fusion | flops 688128 | bytes 918528 | tf_op jit(solution)/shard_map/convert_element_type | solution.py:253
  32.2 12.0 %collective-permute-done.17 = bf16[96,640]{1,0:T(8,128)(2,1)S(1)} collective-permute-done((bf16[96,640]{1,0:T(8,128)(2,1)}, bf16[96,640]{1,0:T(8,128)(2,1)S(1)}, u32[]{:S(2)}, u32[]{:S(2)}) %collective-permute-start.17) | collective-permute-done | bytes 122912 | tf_op jit(solution)/shard_map/ppermute | solution.py:222
  44.8 0.6 collective-permute-start.20
  45.4 1.5 collective-permute-start.2
  47.4 1.3 select_select_fusion.3
  48.7 3.7 %collective-permute-done.2 = bf16[320,256]{1,0:T(8,128)(2,1)S(1)} collective-permute-done((bf16[320,256]{1,0:T(8,128)(2,1)S(1)}, bf16[320,256]{1,0:T(8,128)(2,1)S(1)}, u32[]{:S(2)}, u32[]{:S(2)}) %collective-permute-start.2) | collective-permute-done | bytes 163872 | tf_op jit(solution)/shard_map/ppermute | solution.py:223
  52.5 2.3 %collective-permute-done.4 = bf16[320,256]{1,0:T(8,128)(2,1)S(1)} collective-permute-done((bf16[320,256]{1,0:T(8,128)(2,1)}, bf16[320,256]{1,0:T(8,128)(2,1)S(1)}, u32[]{:S(2)}, u32[]{:S(2)}) %collective-permute-start.4) | collective-permute-done | bytes 163872 | tf_op jit(solution)/shard_map/ppermute | solution.py:223
  54.7 1.5 collective-permute-start.18
  56.3 1.0 select_select_fusion.7
  57.4 4.1 %collective-permute-done.20.refs_6_ = bf16[256,1280]{1,0:T(8,128)(2,1)S(1)} collective-permute-done((bf16[256,1280]{1,0:T(8,128)(2,1)S(1)}, bf16[256,1280]{1,0:T(8,128)(2,1)S(1)}, u32[]{:S(2)}, u32[]{:S(2)}) %collective-permute-start.20) | collective-permute-done | bytes 655392 | tf_op jit(solution)/shard_map/ppermute | solution.py:222
  61.5 5.2 %collective-permute-done.18 = bf16[384,640]{1,0:T(8,128)(2,1)S(1)} collective-permute-done((bf16[384,640]{1,0:T(8,128)(2,1)S(1)}, bf16[384,640]{1,0:T(8,128)(2,1)S(1)}, u32[]{:S(2)}, u32[]{:S(2)}) %collective-permute-start.18) | collective-permute-done | bytes 491552 | tf_op jit(solution)/shard_map/ppermute | solution.py:223
  67.0 1.6 collective-permute-start.10
  68.6 16.1 %shard_map.129 = (bf16[1280,3456]{1,0:T(8,128)(2,1)}, f32[1280,3456]{1,0:T(8,128)}, f32[1280,3456]{1,0:T(8,128)}) custom-call(bf16[1280,256]{1,0:T(8,128)(2,1)S(1)} %bitcast.28, bf16[1280,256]{1,0:T(8,128)(2,1)S(1)} %collective-permute-done.refs_1_, bf16[1280,256]{1,0:T(8,128)(2,1)S(1)} %get-tuple-element.72.refs_2_, ...), custom_call_target="tpu_custom_call" | custom-call | flops 3355443200 | bytes 32768000 | tf_op jit(solution)/shard_map/pallas_call | solution.py:107
  84.8 18.0 %shard_map.130 = (bf16[1280,3456]{1,0:T(8,128)(2,1)}, f32[1280,3456]{1,0:T(8,128)}, f32[1280,3456]{1,0:T(8,128)}, bf16[2,192,1280]{2,1,0:T(8,128)(2,1)S(1)}, bf16[2,192,1280]{2,1,0:T(8,128)(2,1)S(1)}) custom-call(bf16[1280,256]{1,0:T(8,128)(2,1)S(1)} %bitcast.29, ...), custom_call_target="tpu_custom_call", output_to_operand_aliasing={{0}: (12, {}), {1}: (13, {}), {2}: (14, {})} | custom-call | flops 5872025600 | bytes 32768000 | tf_op jit(solution)/shard_map/pallas_call | solution.py:107
  103.5 2.5 %collective-permute-done.9.refs_5_ = bf16[256,896]{1,0:T(8,128)(2,1)S(1)} collective-permute-done((bf16[256,896]{1,0:T(8,128)(2,1)S(1)}, bf16[256,896]{1,0:T(8,128)(2,1)S(1)}, u32[]{:S(2)}, u32[]{:S(2)}) %collective-permute-start.9) | collective-permute-done | bytes 458784 | tf_op jit(solution)/shard_map/ppermute | solution.py:222
  106.0 0.7 collective-permute-done.11.refs_7_
  106.6 12.0 %shard_map.131 = (bf16[1280,3456]{1,0:T(8,128)(2,1)}, f32[1280,3456]{1,0:T(8,128)}, f32[1280,3456]{1,0:T(8,128)}, bf16[1,192,896]{2,1,0:T(8,128)(2,1)S(1)}, bf16[1,192,896]{2,1,0:T(8,128)(2,1)S(1)}) custom-call(bf16[1280,256]{1,0:T(8,128)(2,1)S(1)} %bitcast.30, ...), custom_call_target="tpu_custom_call", output_to_operand_aliasing={{0}: (12, {}), {1}: (13, {}), {2}: (14, {})} | custom-call | flops 3229614080 | bytes 22937600 | tf_op jit(solution)/shard_map/pallas_call | solution.py:107
  119.1 0.8 slice.138
  120.6 1.0 convert_add_fusion.1
  121.7 1.5 collective-permute-start.26
  123.2 11.2 %collective-permute-done.29 = bf16[2,96,1280]{2,1,0:T(8,128)(2,1)} collective-permute-done((bf16[2,96,1280]{2,1,0:T(8,128)(2,1)}, bf16[2,96,1280]{2,1,0:T(8,128)(2,1)}, u32[]{:S(2)}, u32[]{:S(2)}) %collective-permute-start.29) | collective-permute-done | bytes 491552 | tf_op jit(solution)/shard_map/ppermute | solution.py:222
  134.4 1.3 multiply_convert_fusion.2
  135.7 1.5 collective-permute-done.26
  137.6 8.3 %shard_map.132.refs_5_ = f32[192,2560]{1,0:T(8,128)S(1)} custom-call(s32[2]{0:T(128)S(1)} %pad_add_fusion.refs_0_, bf16[96,1280]{1,0:T(8,128)(2,1)S(1)} %get-tuple-element.65.refs_1_, bf16[96,1280]{1,0:T(8,128)(2,1)S(1)} %get-tuple-element.64.refs_2_, bf16[96,1280]{1,0:T(8,128)(2,1)S(1)} %get-tuple-element.63.refs_3_, ...), custom_call_target="tpu_custom_call" | custom-call | flops 2516582400 | bytes 13107200 | tf_op jit(solution)/shard_map/pallas_call | solution.py:180
  146.0 5.1 %shard_map.133 = (bf16[96,2560]{1,0:T(8,128)(2,1)S(1)}, bf16[96,2560]{1,0:T(8,128)(2,1)S(1)}) custom-call(s32[2]{0:T(128)S(1)} %pad_add_fusion.refs_0_, bf16[96,896]{1,0:T(8,128)(2,1)S(1)} %fusion.refs_1_, bf16[96,896]{1,0:T(8,128)(2,1)S(1)} %collective-permute-done.27.refs_2_, bf16[5120,3456]{1,0:T(8,128)(2,1)} %refs_4_.1, bf16[5120,3456]{1,0:T(8,128)(2,1)} %refs_4_.1, ...), custom_call_target="tpu_custom_call" | custom-call | flops 880803840 | bytes 4587520 | tf_op jit(solution)/shard_map/pallas_call | solution.py:180
  151.6 1.6 collective-permute-start.31
  153.2 6.2 %collective-permute-done.34 = bf16[96,1280]{1,0:T(8,128)(2,1)S(1)} collective-permute-done((bf16[96,1280]{1,0:T(8,128)(2,1)S(1)}, bf16[96,1280]{1,0:T(8,128)(2,1)S(1)}, u32[]{:S(2)}, u32[]{:S(2)}) %collective-permute-start.34) | collective-permute-done | bytes 245792 | tf_op jit(solution)/shard_map/ppermute | solution.py:223
  159.5 1.7 collective-permute-start.35
  161.7 2.8 %collective-permute-done.35 = bf16[96,640]{1,0:T(8,128)(2,1)S(1)} collective-permute-done((bf16[96,640]{1,0:T(8,128)(2,1)S(1)}, bf16[96,640]{1,0:T(8,128)(2,1)S(1)}, u32[]{:S(2)}, u32[]{:S(2)}) %collective-permute-start.35) | collective-permute-done | bytes 122912 | tf_op jit(solution)/shard_map/ppermute | solution.py:223
  164.6 1.9 %collective-permute-start.36 = (bf16[96,320]{1,0:T(8,128)(2,1)S(1)}, bf16[96,320]{1,0:T(8,128)(2,1)S(1)}, u32[]{:S(2)}, u32[]{:S(2)}) collective-permute-start(bf16[96,320]{1,0:T(8,128)(2,1)S(1)} %slice.110), channel_id=1, source_target_pairs={{0,4},{1,5},{2,6},{3,7},{4,0},{5,1},{6,2},{7,3},{8,12},{9,13},{10,... | collective-permute-start | bytes 184328 | tf_op jit(solution)/shard_map/ppermute | solution.py:223
  166.6 2.2 %collective-permute-start.33 = (bf16[96,320]{1,0:T(8,128)(2,1)S(1)}, bf16[96,320]{1,0:T(8,128)(2,1)S(1)}, u32[]{:S(2)}, u32[]{:S(2)}) collective-permute-start(bf16[96,320]{1,0:T(8,128)(2,1)S(1)} %slice.106), channel_id=1, source_target_pairs={{0,4},{1,5},{2,6},{3,7},{4,0},{5,1},{6,2},{7,3},{8,12},{9,13},{10,... | collective-permute-start | bytes 184328 | tf_op jit(solution)/shard_map/ppermute | solution.py:223
  168.8 2.7 %collective-permute-done.36 = bf16[96,320]{1,0:T(8,128)(2,1)S(1)} collective-permute-done((bf16[96,320]{1,0:T(8,128)(2,1)S(1)}, bf16[96,320]{1,0:T(8,128)(2,1)S(1)}, u32[]{:S(2)}, u32[]{:S(2)}) %collective-permute-start.36) | collective-permute-done | bytes 61472 | tf_op jit(solution)/shard_map/ppermute | solution.py:223
  171.6 1.5 collective-permute-done.33
  173.1 1.0 convolution_convert_fusion
  (89 shorter events, 6.8 us)
Async XLA Ops:
  0.6 3.4 %copy-start = (bf16[128,640]{1,0:T(8,128)(2,1)S(1)}, bf16[128,640]{1,0:T(8,128)(2,1)}, u32[]{:S(2)}) copy-start(bf16[128,640]{1,0:T(8,128)(2,1)} %param.17) | copy-start | bytes 491524
  0.6 11.0 %copy-start.4 = (s32[1,256]{1,0:T(1,128)S(1)}, s32[1,256]{1,0:T(1,128)}, u32[]{:S(2)}) copy-start(s32[1,256]{1,0:T(1,128)} %param.12) | copy-start | bytes 3076
  0.7 3.2 %copy-start.5 = (s32[1,4]{1,0:T(1,128)S(1)}, s32[1,4]{1,0:T(1,128)}, u32[]{:S(2)}) copy-start(s32[1,4]{1,0:T(1,128)} %param.19) | copy-start | bytes 52
  0.7 11.1 %copy-start.6 = (f32[1,8]{1,0:T(1,128)S(1)}, f32[1,8]{1,0:T(1,128)}, u32[]{:S(2)}) copy-start(f32[1,8]{1,0:T(1,128)} %param.13) | copy-start | bytes 100
  4.2 7.8 %collective-permute-start.12 = (bf16[96,640]{1,0:T(8,128)(2,1)S(1)}, bf16[96,640]{1,0:T(8,128)(2,1)S(1)}, u32[]{:S(2)}, u32[]{:S(2)}) collective-permute-start(bf16[96,640]{1,0:T(8,128)(2,1)S(1)} %convolution_convert_fusion.1), channel_id=1, source_target_pairs={{0,2},{1,3},{2,0},{3,1},{4,6},{5,7},{6,4},{7,5},{8,10},{9,11},{10,... | collective-permute-start | bytes 368648 | tf_op jit(solution)/shard_map/ppermute | solution.py:223
  7.4 12.3 %collective-permute-start.13 = (bf16[96,640]{1,0:T(8,128)(2,1)S(1)}, bf16[96,640]{1,0:T(8,128)(2,1)S(1)}, u32[]{:S(2)}, u32[]{:S(2)}) collective-permute-start(bf16[96,640]{1,0:T(8,128)(2,1)S(1)} %convolution_convert_fusion.1), channel_id=1, source_target_pairs={{0,4},{1,5},{2,6},{3,7},{4,0},{5,1},{6,2},{7,3},{8,12},{9,13},{10,... | collective-permute-start | bytes 368648 | tf_op jit(solution)/shard_map/ppermute | solution.py:223
  9.9 9.7 %collective-permute-start.14 = (bf16[96,640]{1,0:T(8,128)(2,1)S(1)}, bf16[96,640]{1,0:T(8,128)(2,1)S(1)}, u32[]{:S(2)}, u32[]{:S(2)}) collective-permute-start(bf16[96,640]{1,0:T(8,128)(2,1)S(1)} %convolution_convert_fusion.1), channel_id=1, source_target_pairs={{0,6},{1,7},{2,4},{3,5},{4,2},{5,3},{6,0},{7,1},{8,14},{9,15},{10,... | collective-permute-start | bytes 368648 | tf_op jit(solution)/shard_map/ppermute | solution.py:223
  9.9 12.0 %collective-permute-start.5 = (bf16[320,256]{1,0:T(8,128)(2,1)S(1)}, bf16[320,256]{1,0:T(8,128)(2,1)S(1)}, u32[]{:S(2)}, u32[]{:S(2)}) collective-permute-start(bf16[320,256]{1,0:T(8,128)(2,1)S(1)} %get-tuple-element.26), channel_id=1, source_target_pairs={{0,24},{8,16},{16,8},{24,0},{1,25},{9,17},{17,9},{25,1},{2,26},{10... | collective-permute-start | bytes 491528 | tf_op jit(solution)/shard_map/ppermute | solution.py:222
  10.3 15.6 %collective-permute-start.1 = (bf16[320,256]{1,0:T(8,128)(2,1)}, bf16[320,256]{1,0:T(8,128)(2,1)S(1)}, u32[]{:S(2)}, u32[]{:S(2)}) collective-permute-start(bf16[320,256]{1,0:T(8,128)(2,1)} %get-tuple-element.25), channel_id=1, source_target_pairs={{0,16},{8,24},{16,0},{24,8},{1,17},{9,25},{17,1},{25,9},{2,18},{10... | collective-permute-start | bytes 491528 | tf_op jit(solution)/shard_map/ppermute | solution.py:222
  20.4 6.6 %collective-permute-start.15 = (bf16[96,640]{1,0:T(8,128)(2,1)S(1)}, bf16[96,640]{1,0:T(8,128)(2,1)S(1)}, u32[]{:S(2)}, u32[]{:S(2)}) collective-permute-start(bf16[96,640]{1,0:T(8,128)(2,1)S(1)} %get-tuple-element.69), channel_id=1, source_target_pairs={{0,16},{8,24},{16,0},{24,8},{1,17},{9,25},{17,1},{25,9},{2,18},{10... | collective-permute-start | bytes 368648 | tf_op jit(solution)/shard_map/ppermute | solution.py:222
  21.9 6.6 %collective-permute-start.16 = (bf16[96,640]{1,0:T(8,128)(2,1)S(1)}, bf16[96,640]{1,0:T(8,128)(2,1)S(1)}, u32[]{:S(2)}, u32[]{:S(2)}) collective-permute-start(bf16[96,640]{1,0:T(8,128)(2,1)S(1)} %get-tuple-element.68), channel_id=1, source_target_pairs={{0,8},{8,0},{16,24},{24,16},{1,9},{9,1},{17,25},{25,17},{2,10},{10... | collective-permute-start | bytes 368648 | tf_op jit(solution)/shard_map/ppermute | solution.py:222
  21.9 6.9 %collective-permute-start.7 = (bf16[320,256]{1,0:T(8,128)(2,1)S(1)}, bf16[320,256]{1,0:T(8,128)(2,1)}, u32[]{:S(2)}, u32[]{:S(2)}) collective-permute-start(bf16[320,256]{1,0:T(8,128)(2,1)S(1)} %collective-permute-done.5), channel_id=1, source_target_pairs={{0,2},{1,3},{2,0},{3,1},{4,6},{5,7},{6,4},{7,5},{8,10},{9,11},{10,... | collective-permute-start | bytes 491528 | tf_op jit(solution)/shard_map/ppermute | solution.py:223
  25.4 31.9 %collective-permute-start.23 = (bf16[256,1280]{1,0:T(8,128)(2,1)S(1)}, bf16[256,1280]{1,0:T(8,128)(2,1)}, u32[]{:S(2)}, u32[]{:S(2)}) collective-permute-start(bf16[256,1280]{1,0:T(8,128)(2,1)S(1)} %get-tuple-element.50.refs_4_), channel_id=1, source_target_pairs={{0,16},{8,24},{16,0},{24,8},{1,17},{9,25},{17,1},{25,9},{2,18},{10... | collective-permute-start | bytes 1966088 | tf_op jit(solution)/shard_map/ppermute | solution.py:222
  26.0 18.2 %collective-permute-start.17 = (bf16[96,640]{1,0:T(8,128)(2,1)}, bf16[96,640]{1,0:T(8,128)(2,1)S(1)}, u32[]{:S(2)}, u32[]{:S(2)}) collective-permute-start(bf16[96,640]{1,0:T(8,128)(2,1)} %get-tuple-element.67), channel_id=1, source_target_pairs={{0,24},{8,16},{16,8},{24,0},{1,25},{9,17},{17,9},{25,1},{2,26},{10... | collective-permute-start | bytes 368648 | tf_op jit(solution)/shard_map/ppermute | solution.py:222
  27.0 17.8 %collective-permute-start.6 = (bf16[320,256]{1,0:T(8,128)(2,1)S(1)}, bf16[320,256]{1,0:T(8,128)(2,1)}, u32[]{:S(2)}, u32[]{:S(2)}) collective-permute-start(bf16[320,256]{1,0:T(8,128)(2,1)S(1)} %collective-permute-done.5), channel_id=1, source_target_pairs={{0,1},{1,0},{2,3},{3,2},{4,5},{5,4},{6,7},{7,6},{8,9},{9,8},{10,11... | collective-permute-start | bytes 491528 | tf_op jit(solution)/shard_map/ppermute | solution.py:223
  28.5 16.9 %collective-permute-start.3 = (bf16[320,256]{1,0:T(8,128)(2,1)S(1)}, bf16[320,256]{1,0:T(8,128)(2,1)}, u32[]{:S(2)}, u32[]{:S(2)}) collective-permute-start(bf16[320,256]{1,0:T(8,128)(2,1)S(1)} %collective-permute-done.1), channel_id=1, source_target_pairs={{0,2},{1,3},{2,0},{3,1},{4,6},{5,7},{6,4},{7,5},{8,10},{9,11},{10,... | collective-permute-start | bytes 491528 | tf_op jit(solution)/shard_map/ppermute | solution.py:223
  28.8 18.1 %collective-permute-start.8 = (bf16[320,256]{1,0:T(8,128)(2,1)}, bf16[320,256]{1,0:T(8,128)(2,1)}, u32[]{:S(2)}, u32[]{:S(2)}) collective-permute-start(bf16[320,256]{1,0:T(8,128)(2,1)} %collective-permute-done.7), channel_id=1, source_target_pairs={{0,1},{1,0},{2,3},{3,2},{4,5},{5,4},{6,7},{7,6},{8,9},{9,8},{10,11... | collective-permute-start | bytes 491528 | tf_op jit(solution)/shard_map/ppermute | solution.py:223
  44.2 22.8 %collective-permute-start.22 = (bf16[256,1280]{1,0:T(8,128)(2,1)S(1)}, bf16[256,1280]{1,0:T(8,128)(2,1)S(1)}, u32[]{:S(2)}, u32[]{:S(2)}) collective-permute-start(bf16[256,1280]{1,0:T(8,128)(2,1)S(1)} %get-tuple-element.50.refs_4_), channel_id=1, source_target_pairs={{0,8},{8,0},{16,24},{24,16},{1,9},{9,1},{17,25},{25,17},{2,10},{10... | collective-permute-start | bytes 1966088 | tf_op jit(solution)/shard_map/ppermute | solution.py:222
  44.7 22.3 %copy-start.3 = (bf16[256,896]{1,0:T(8,128)(2,1)S(1)}, bf16[256,896]{1,0:T(8,128)(2,1)}, u32[]{:S(2)}) copy-start(bf16[256,896]{1,0:T(8,128)(2,1)} %multiply_convert_fusion.3.refs_4_) | copy-start | bytes 1376260
  44.8 16.7 %collective-permute-start.20 = (bf16[256,1280]{1,0:T(8,128)(2,1)S(1)}, bf16[256,1280]{1,0:T(8,128)(2,1)S(1)}, u32[]{:S(2)}, u32[]{:S(2)}) collective-permute-start(bf16[256,1280]{1,0:T(8,128)(2,1)S(1)} %get-tuple-element.51.refs_4_), channel_id=1, source_target_pairs={{0,16},{8,24},{16,0},{24,8},{1,17},{9,25},{17,1},{25,9},{2,18},{10... | collective-permute-start | bytes 1966088 | tf_op jit(solution)/shard_map/ppermute | solution.py:222
  45.4 7.1 %collective-permute-start.2 = (bf16[320,256]{1,0:T(8,128)(2,1)S(1)}, bf16[320,256]{1,0:T(8,128)(2,1)S(1)}, u32[]{:S(2)}, u32[]{:S(2)}) collective-permute-start(bf16[320,256]{1,0:T(8,128)(2,1)S(1)} %collective-permute-done.1), channel_id=1, source_target_pairs={{0,1},{1,0},{2,3},{3,2},{4,5},{5,4},{6,7},{7,6},{8,9},{9,8},{10,11... | collective-permute-start | bytes 491528 | tf_op jit(solution)/shard_map/ppermute | solution.py:223
  46.9 7.8 %collective-permute-start.4 = (bf16[320,256]{1,0:T(8,128)(2,1)}, bf16[320,256]{1,0:T(8,128)(2,1)S(1)}, u32[]{:S(2)}, u32[]{:S(2)}) collective-permute-start(bf16[320,256]{1,0:T(8,128)(2,1)} %collective-permute-done.3), channel_id=1, source_target_pairs={{0,1},{1,0},{2,3},{3,2},{4,5},{5,4},{6,7},{7,6},{8,9},{9,8},{10,11... | collective-permute-start | bytes 491528 | tf_op jit(solution)/shard_map/ppermute | solution.py:223
  47.4 21.2 %copy-start.2 = (bf16[1280,3456]{1,0:T(8,128)(2,1)S(1)}, bf16[1280,3456]{1,0:T(8,128)(2,1)}, u32[]{:S(2)}) copy-start(bf16[1280,3456]{1,0:T(8,128)(2,1)} %refs_8_.5) | copy-start | bytes 26542084
  52.5 16.1 %collective-permute-start = (bf16[1280,256]{1,0:T(8,128)(2,1)S(1)}, bf16[1280,256]{1,0:T(8,128)(2,1)S(1)}, u32[]{:S(2)}, u32[]{:S(2)}) collective-permute-start(bf16[1280,256]{1,0:T(8,128)(2,1)S(1)} %bitcast.33), channel_id=1, source_target_pairs={{0,8},{8,0},{16,24},{24,16},{1,9},{9,1},{17,25},{25,17},{2,10},{10... | collective-permute-start | bytes 1966088 | tf_op jit(solution)/shard_map/ppermute | solution.py:222
  54.7 12.0 %collective-permute-start.18 = (bf16[384,640]{1,0:T(8,128)(2,1)S(1)}, bf16[384,640]{1,0:T(8,128)(2,1)S(1)}, u32[]{:S(2)}, u32[]{:S(2)}) collective-permute-start(bf16[384,640]{1,0:T(8,128)(2,1)S(1)} %pad_maximum_fusion.3), channel_id=1, source_target_pairs={{0,1},{1,0},{2,3},{3,2},{4,5},{5,4},{6,7},{7,6},{8,9},{9,8},{10,11... | collective-permute-start | bytes 1474568 | tf_op jit(solution)/shard_map/ppermute | solution.py:223
  57.3 11.3 %collective-permute-start.24 = (bf16[256,1280]{1,0:T(8,128)(2,1)}, bf16[256,1280]{1,0:T(8,128)(2,1)S(1)}, u32[]{:S(2)}, u32[]{:S(2)}) collective-permute-start(bf16[256,1280]{1,0:T(8,128)(2,1)} %collective-permute-done.23.refs_6_), channel_id=1, source_target_pairs={{0,8},{8,0},{16,24},{24,16},{1,9},{9,1},{17,25},{25,17},{2,10},{10... | collective-permute-start | bytes 1966088 | tf_op jit(solution)/shard_map/ppermute | solution.py:222
  61.5 23.2 %collective-permute-start.19 = (bf16[256,1280]{1,0:T(8,128)(2,1)S(1)}, bf16[256,1280]{1,0:T(8,128)(2,1)S(1)}, u32[]{:S(2)}, u32[]{:S(2)}) collective-permute-start(bf16[256,1280]{1,0:T(8,128)(2,1)S(1)} %get-tuple-element.51.refs_4_), channel_id=1, source_target_pairs={{0,8},{8,0},{16,24},{24,16},{1,9},{9,1},{17,25},{25,17},{2,10},{10... | collective-permute-start | bytes 1966088 | tf_op jit(solution)/shard_map/ppermute | solution.py:222
  66.7 18.0 %collective-permute-start.21 = (bf16[256,1280]{1,0:T(8,128)(2,1)S(1)}, bf16[256,1280]{1,0:T(8,128)(2,1)S(1)}, u32[]{:S(2)}, u32[]{:S(2)}) collective-permute-start(bf16[256,1280]{1,0:T(8,128)(2,1)S(1)} %collective-permute-done.20.refs_6_), channel_id=1, source_target_pairs={{0,8},{8,0},{16,24},{24,16},{1,9},{9,1},{17,25},{25,17},{2,10},{10... | collective-permute-start | bytes 1966088 | tf_op jit(solution)/shard_map/ppermute | solution.py:222
  67.0 36.3 %collective-permute-start.10 = (bf16[256,896]{1,0:T(8,128)(2,1)S(1)}, bf16[256,896]{1,0:T(8,128)(2,1)S(1)}, u32[]{:S(2)}, u32[]{:S(2)}) collective-permute-start(bf16[256,896]{1,0:T(8,128)(2,1)S(1)} %copy-done.3), channel_id=1, source_target_pairs={{0,16},{8,24},{16,0},{24,8},{1,17},{9,25},{17,1},{25,9},{2,18},{10... | collective-permute-start | bytes 1376264 | tf_op jit(solution)/shard_map/ppermute | solution.py:222
  102.8 16.1 %collective-permute-start.28 = (bf16[2,192,1280]{2,1,0:T(8,128)(2,1)S(1)}, bf16[2,192,1280]{2,1,0:T(8,128)(2,1)S(1)}, u32[]{:S(2)}, u32[]{:S(2)}) collective-permute-start(bf16[2,192,1280]{2,1,0:T(8,128)(2,1)S(1)} %get-tuple-element.41), channel_id=1, source_target_pairs={{0,8},{8,0},{16,24},{24,16},{1,9},{9,1},{17,25},{25,17},{2,10},{10... | collective-permute-start | bytes 2949128 | tf_op jit(solution)/shard_map/ppermute | solution.py:222
  103.0 3.0 %collective-permute-start.9 = (bf16[256,896]{1,0:T(8,128)(2,1)S(1)}, bf16[256,896]{1,0:T(8,128)(2,1)S(1)}, u32[]{:S(2)}, u32[]{:S(2)}) collective-permute-start(bf16[256,896]{1,0:T(8,128)(2,1)S(1)} %copy-done.3), channel_id=1, source_target_pairs={{0,8},{8,0},{16,24},{24,16},{1,9},{9,1},{17,25},{25,17},{2,10},{10... | collective-permute-start | bytes 1376264 | tf_op jit(solution)/shard_map/ppermute | solution.py:222
  103.3 3.4 %collective-permute-start.11 = (bf16[256,896]{1,0:T(8,128)(2,1)S(1)}, bf16[256,896]{1,0:T(8,128)(2,1)S(1)}, u32[]{:S(2)}, u32[]{:S(2)}) collective-permute-start(bf16[256,896]{1,0:T(8,128)(2,1)S(1)} %collective-permute-done.10.refs_6_), channel_id=1, source_target_pairs={{0,8},{8,0},{16,24},{24,16},{1,9},{9,1},{17,25},{25,17},{2,10},{10... | collective-permute-start | bytes 1376264 | tf_op jit(solution)/shard_map/ppermute | solution.py:222
  118.7 2.0 %collective-permute-start.25 = (bf16[1,192,896]{2,1,0:T(8,128)(2,1)S(1)}, bf16[1,192,896]{2,1,0:T(8,128)(2,1)}, u32[]{:S(2)}, u32[]{:S(2)}) collective-permute-start(bf16[1,192,896]{2,1,0:T(8,128)(2,1)S(1)} %get-tuple-element.39), channel_id=1, source_target_pairs={{0,8},{8,0},{16,24},{24,16},{1,9},{9,1},{17,25},{25,17},{2,10},{10... | collective-permute-start | bytes 1032200 | tf_op jit(solution)/shard_map/ppermute | solution.py:222
  119.9 14.4 %collective-permute-start.29 = (bf16[2,96,1280]{2,1,0:T(8,128)(2,1)}, bf16[2,96,1280]{2,1,0:T(8,128)(2,1)}, u32[]{:S(2)}, u32[]{:S(2)}) collective-permute-start(bf16[2,96,1280]{2,1,0:T(8,128)(2,1)} %slice.138), channel_id=1, source_target_pairs={{0,16},{8,24},{16,0},{24,8},{1,17},{9,25},{17,1},{25,9},{2,18},{10... | collective-permute-start | bytes 1474568 | tf_op jit(solution)/shard_map/ppermute | solution.py:222
  121.7 15.5 %collective-permute-start.26 = (bf16[1,96,896]{2,1,0:T(8,128)(2,1)S(1)}, bf16[1,96,896]{2,1,0:T(8,128)(2,1)S(1)}, u32[]{:S(2)}, u32[]{:S(2)}) collective-permute-start(bf16[1,96,896]{2,1,0:T(8,128)(2,1)S(1)} %slice.139), channel_id=1, source_target_pairs={{0,16},{8,24},{16,0},{24,8},{1,17},{9,25},{17,1},{25,9},{2,18},{10... | collective-permute-start | bytes 516104 | tf_op jit(solution)/shard_map/ppermute | solution.py:222
  135.7 1.9 %collective-permute-start.30 = (bf16[2,96,1280]{2,1,0:T(8,128)(2,1)S(1)}, bf16[2,96,1280]{2,1,0:T(8,128)(2,1)S(1)}, u32[]{:S(2)}, u32[]{:S(2)}) collective-permute-start(bf16[2,96,1280]{2,1,0:T(8,128)(2,1)S(1)} %multiply_convert_fusion.2), channel_id=1, source_target_pairs={{0,8},{8,0},{16,24},{24,16},{1,9},{9,1},{17,25},{25,17},{2,10},{10... | collective-permute-start | bytes 1474568 | tf_op jit(solution)/shard_map/ppermute | solution.py:222
  137.3 8.6 %collective-permute-start.27 = (bf16[96,896]{1,0:T(8,128)(2,1)S(1)}, bf16[96,896]{1,0:T(8,128)(2,1)S(1)}, u32[]{:S(2)}, u32[]{:S(2)}) collective-permute-start(bf16[96,896]{1,0:T(8,128)(2,1)S(1)} %fusion.refs_1_), channel_id=1, source_target_pairs={{0,8},{8,0},{16,24},{24,16},{1,9},{9,1},{17,25},{25,17},{2,10},{10... | collective-permute-start | bytes 516104 | tf_op jit(solution)/shard_map/ppermute | solution.py:222
  151.1 8.3 %collective-permute-start.34 = (bf16[96,1280]{1,0:T(8,128)(2,1)S(1)}, bf16[96,1280]{1,0:T(8,128)(2,1)S(1)}, u32[]{:S(2)}, u32[]{:S(2)}) collective-permute-start(bf16[96,1280]{1,0:T(8,128)(2,1)S(1)} %slice.90), channel_id=1, source_target_pairs={{0,2},{1,3},{2,0},{3,1},{4,6},{5,7},{6,4},{7,5},{8,10},{9,11},{10,... | collective-permute-start | bytes 737288 | tf_op jit(solution)/shard_map/ppermute | solution.py:223
  151.6 22.5 %copy-start.1 = (bf16[128,640]{1,0:T(8,128)(2,1)S(1)}, bf16[128,640]{1,0:T(8,128)(2,1)}, u32[]{:S(2)}) copy-start(bf16[128,640]{1,0:T(8,128)(2,1)} %param.17) | copy-start | bytes 491524
  151.6 9.6 %collective-permute-start.31 = (bf16[96,1280]{1,0:T(8,128)(2,1)S(1)}, bf16[96,1280]{1,0:T(8,128)(2,1)S(1)}, u32[]{:S(2)}, u32[]{:S(2)}) collective-permute-start(bf16[96,1280]{1,0:T(8,128)(2,1)S(1)} %slice.84), channel_id=1, source_target_pairs={{0,1},{1,0},{2,3},{3,2},{4,5},{5,4},{6,7},{7,6},{8,9},{9,8},{10,11... | collective-permute-start | bytes 737288 | tf_op jit(solution)/shard_map/ppermute | solution.py:223
  159.5 4.9 %collective-permute-start.35 = (bf16[96,640]{1,0:T(8,128)(2,1)S(1)}, bf16[96,640]{1,0:T(8,128)(2,1)S(1)}, u32[]{:S(2)}, u32[]{:S(2)}) collective-permute-start(bf16[96,640]{1,0:T(8,128)(2,1)S(1)} %slice.108), channel_id=1, source_target_pairs={{0,1},{1,0},{2,3},{3,2},{4,5},{5,4},{6,7},{7,6},{8,9},{9,8},{10,11... | collective-permute-start | bytes 368648 | tf_op jit(solution)/shard_map/ppermute | solution.py:223
  161.3 5.2 %collective-permute-start.32 = (bf16[96,640]{1,0:T(8,128)(2,1)S(1)}, bf16[96,640]{1,0:T(8,128)(2,1)S(1)}, u32[]{:S(2)}, u32[]{:S(2)}) collective-permute-start(bf16[96,640]{1,0:T(8,128)(2,1)S(1)} %slice.104), channel_id=1, source_target_pairs={{0,2},{1,3},{2,0},{3,1},{4,6},{5,7},{6,4},{7,5},{8,10},{9,11},{10,... | collective-permute-start | bytes 368648 | tf_op jit(solution)/shard_map/ppermute | solution.py:223
  164.6 6.9 %collective-permute-start.36 = (bf16[96,320]{1,0:T(8,128)(2,1)S(1)}, bf16[96,320]{1,0:T(8,128)(2,1)S(1)}, u32[]{:S(2)}, u32[]{:S(2)}) collective-permute-start(bf16[96,320]{1,0:T(8,128)(2,1)S(1)} %slice.110), channel_id=1, source_target_pairs={{0,4},{1,5},{2,6},{3,7},{4,0},{5,1},{6,2},{7,3},{8,12},{9,13},{10,... | collective-permute-start | bytes 184328 | tf_op jit(solution)/shard_map/ppermute | solution.py:223
  166.6 6.5 %collective-permute-start.33 = (bf16[96,320]{1,0:T(8,128)(2,1)S(1)}, bf16[96,320]{1,0:T(8,128)(2,1)S(1)}, u32[]{:S(2)}, u32[]{:S(2)}) collective-permute-start(bf16[96,320]{1,0:T(8,128)(2,1)S(1)} %slice.106), channel_id=1, source_target_pairs={{0,4},{1,5},{2,6},{3,7},{4,0},{5,1},{6,2},{7,3},{8,12},{9,13},{10,... | collective-permute-start | bytes 184328 | tf_op jit(solution)/shard_map/ppermute | solution.py:223
  171.5 1.6 collective-permute-start.37
where the time goes:
time: 175 us; the launch traced here: 174 us
  waiting for transfers between devices  64.1 us (37%)
  Pallas kernels  59.6 us (34%)
  starting transfers between devices  33.6 us (19%)
  other arithmetic  10.3 us (6%)
  local copies, waits for them, and re-layouts  4.3 us (2%)
    pallas_call x3, Pallas kernels, adam_chunk(): pl.pallas_call(functools.partial(adam_kernel, lanes, bool(chain), previou...  46.2 us
    ppermute x16, waiting for transfers between devices, inner(): swap_col = lambda a, bit: lax.ppermute(a, 'col', xor_pairs(cols, bit))  32.1 us
    ppermute x22, waiting for transfers between devices, inner(): swap_rep = lambda a, bit: lax.ppermute(a, 'rep', xor_pairs(reps, bit))  32 us
    ppermute x16, starting transfers between devices, inner(): swap_col = lambda a, bit: lax.ppermute(a, 'col', xor_pairs(cols, bit))  22.7 us
    pallas_call x2, Pallas kernels, down_part(): pl.pallas_call(functools.partial(down_kernel, groups, past is not None),...  13.4 us
    ppermute x22, starting transfers between devices, inner(): swap_rep = lambda a, bit: lax.ppermute(a, 'rep', xor_pairs(reps, bit))  11 us
  transfers between devices with their start and end apart: 38, of which 16 were waited for; matrix products, arithmetic and copies ran while one was open for 6% of the time, Pallas kernels for 31%

commit v1 on v0

--- a/solution.py
+++ b/solution.py
@@ -13,7 +13,8 @@
 LIVE = 96
 
 
-VMEM_ADAM = 40 * 1024 * 1024
+RESIDENT = ()
+VMEM_ADAM = 31 * 1024 * 1024
 VMEM_DOWN = 32 * 1024 * 1024
 
 first_decay = 0.9
@@ -48,7 +49,7 @@
     return (jnp.arange(LIVE, dtype=jnp.int32)[:, None] == place[None, :]).astype(jnp.bfloat16)
 
 
-def adam_kernel(lanes, chained, previous, own, *refs):
+def adam_kernel(lanes, chained, previous, own, resident, *refs):
     refs = list(refs)
     token_refs, scaled_refs = refs[:lanes], refs[lanes : 2 * lanes]
     w_ref, m_ref, v_ref, x_ref = refs[2 * lanes : 2 * lanes + 4]
@@ -56,7 +57,10 @@
     past_w = refs[0] if chained else None
     new_w, new_m, new_v, *products = refs[3 if chained else 0 :]
     scaled = jnp.concatenate([ref[...] for ref in scaled_refs], axis=0)
-    high = new_w.shape[0]
+    high, tile = new_w.shape
+    if resident:
+        here = pl.ds(pl.multiple_of(pl.program_id(0) * tile, tile), tile)
+        w_ref, m_ref, v_ref = w_ref.at[:, here], m_ref.at[:, here], v_ref.at[:, here]
     part = 256 if high % 256 == 0 else high
     for top in range(0, high, part):
         span = slice(top, top + part)
@@ -78,16 +82,21 @@
         send_ref[k] = value[half:].astype(send_ref.dtype)
 
 
-def adam_chunk(tokens, scaled, weight, first, second, rows, chain, start, tile, previous, own):
+def adam_chunk(tokens, scaled, weight, first, second, rows, chain, start, tile, previous, own, resident):
     lanes, width, high = len(tokens), scaled[0].shape[1], weight.shape[0]
     skip = start // tile
     block = pl.BlockSpec((high, tile), lambda i: (0, i + skip))
     whole = lambda a: pl.BlockSpec(a.shape, lambda i: (0, 0))
     x_arg = rows if rows is not None else jnp.zeros((16, 128), jnp.bfloat16)
-    args = [*tokens, *scaled, weight, first, second, x_arg]
+    inputs = [weight, first, second]
+    if resident:
+        inputs = [lax.slice_in_dim(a, start, start + width, axis=1) for a in inputs]
+    else:
+        inputs = [pltpu.with_memory_space_constraint(a, pltpu.HBM) for a in inputs]
+    args = [*tokens, *scaled, *inputs, x_arg]
     specs = [whole(t) for t in tokens]
     specs += [pl.BlockSpec((s.shape[0], tile), lambda i: (0, i)) for s in scaled]
-    specs += [block, block, block, whole(x_arg)]
+    specs += [pl.BlockSpec(memory_space=pltpu.VMEM) if resident else block] * 3 + [whole(x_arg)]
     alias = {}
     for k, c in enumerate(chain or ()):
         alias[len(args)] = k
@@ -105,7 +114,7 @@
         outs += [jax.ShapeDtypeStruct((groups, half, width), jnp.bfloat16)] * 2
         out_specs += [pl.BlockSpec((groups, half, tile), lambda i: (0, 0, i))] * 2
     return pl.pallas_call(
-        functools.partial(adam_kernel, lanes, bool(chain), previous, own),
+        functools.partial(adam_kernel, lanes, bool(chain), previous, own, resident),
         out_shape=outs,
         grid=(pl.cdiv(width, tile),),
         in_specs=specs,
@@ -195,13 +204,11 @@
 
 
 def column_chunks(columns):
-    tile = 256
-    if columns % 128 or columns < 4 * tile:
+    tile = 384
+    if columns % (3 * tile):
         return [(0, columns)], columns
-    tiles = -(-columns // tile)
-    first = -(-tiles * 5 // 14)
-    edges = [0, first * tile, 2 * first * tile, columns]
-    return [(a, b - a) for a, b in zip(edges, edges[1:])], tile
+    width = columns // 3
+    return [(k * width, width) for k in range(3)], tile
 
 
 def inner(
@@ -226,23 +233,18 @@
 
     features, depth = tokens_learn.shape
     high = features // reps
-    quarter = high // 4
-    blocks = tokens_learn.reshape(reps, 4, quarter, depth)
-    part = col & 3
-
-    def piece(j, which):
-        return lax.dynamic_slice(blocks, (rep ^ j, which, 0, 0), (1, 1, quarter, depth))[0, 0]
-
+    blocks = tokens_learn.reshape(reps, 2, high // 2, depth)
+    side = col & 1
     far = range(2, reps)
-    near = lax.dynamic_index_in_dim(blocks, rep ^ 1, 0, keepdims=False).reshape(high, depth)
-    pieces = [piece(j, part) for j in far]
-    pieces, near, sample_ids, live_lengths = lax.optimization_barrier(
-        (pieces, near, sample_ids, live_lengths)
+    pieces = [lax.dynamic_slice(blocks, (rep ^ j, side, 0, 0), (1, 1, high // 2, depth)) for j in far]
+    pieces, blocks, sample_ids, live_lengths = lax.optimization_barrier(
+        (pieces, blocks, sample_ids, live_lengths)
     )
+    whole_block = lambda j: lax.dynamic_index_in_dim(blocks, rep ^ j, 0, keepdims=False)
     straight = {}
     for j in far:
-        straight[j] = swap_rep(pieces[j - 2], j)
-    near = swap_rep(near, 1)
+        straight[j] = swap_rep(pieces[j - 2][0, 0], j)
+    near = swap_rep(whole_block(1).reshape(high, depth), 1)
 
     token_scale = token_scales(sample_ids, advantage)[0]
     columns = cotangent.shape[1]
@@ -256,13 +258,12 @@
                 lanes[j | bit] = swap_rep(value, bit)
         scaled.append([lanes[j] for j in range(reps)])
 
-    tokens = [lax.dynamic_index_in_dim(blocks, rep, 0, keepdims=False).reshape(high, depth), near]
+    tokens = [whole_block(0).reshape(high, depth), near]
     for j in far:
-        second = swap_col(straight[j], 2)
-        third = swap_col(straight[j], 1)
-        fourth = swap_col(second, 1)
-        got = [straight[j], third, second, fourth]
-        tokens.append(jnp.concatenate([lax.select_n(part ^ i, *got) for i in range(4)], axis=0))
+        second = swap_col(straight[j], 1)
+        tokens.append(
+            jnp.concatenate([lax.select_n(side ^ i, straight[j], second) for i in range(2)], axis=0)
+        )
 
     picks = live_picks(live_lengths[0], rollout_rows.shape[0])
     compact = jnp.dot(picks, rollout_rows, preferred_element_type=f32).astype(bf16)
@@ -288,11 +289,12 @@
 
     def reduced(keep, send):
         got = swap_rep(send, 1)
-        value = keep.astype(f32) + got.astype(f32)
+        terms = [keep, got]
         for bit in bits[-2::-1]:
-            half = value.shape[1] // 2
-            got = swap_rep(value[:, half:].astype(bf16), bit)
-            value = value[:, :half] + got.astype(f32)
+            half = terms[0].shape[1] // 2
+            send = sum(t[:, half:].astype(f32) for t in terms).astype(bf16)
+            terms = [t[:, :half] for t in terms] + [swap_rep(send, bit)]
+        value = sum(t.astype(f32) for t in terms)
         return jax.nn.silu(value).astype(bf16)
 
     chain, acts = None, []
@@ -304,6 +306,7 @@
         *out, = adam_chunk(
             tokens, lanes, up_weight, first_moment, second_moment,
             rows if own or previous else None, chain, start, tile, previous, own,
+            not only and index in RESIDENT,
         )
         chain = out[:3]
         if own:
@@ -322,8 +325,9 @@
             got = swap_col(value[:, half:], bit)
             return (value[:, :half].astype(f32) + got.astype(f32)).astype(bf16)
 
-        for one, two in ((1, 2), (2, 1), (4, 4)):
+        for one, two in ((1, 2), (2, 1)):
             own, other = stage(own, one), stage(other, two)
+        own, other = jnp.split(stage(jnp.concatenate([own, other], axis=0), 4), 2, axis=0)
         other = swap_rep(other, 1)
         lower = (rep & 1) == 0
         held = jnp.concatenate([jnp.where(lower, own, other), jnp.where(lower, other, own)], axis=1)

time: 175 us -> 180 us (1.029)
  waiting for transfers between devices: 64.1 us -> 80.5 us
  starting transfers between devices: 33.6 us -> 25.9 us
    ppermute x22, waiting for transfers between devices: 32 us -> 64.8 us  [inner(): swap_rep = lambda a, bit: lax.ppermute(a, 'rep', xor_pairs(reps, bit))]
    ppermute x16 -> x11, waiting for transfers between devices: 32.1 us -> 15.7 us  [inner(): swap_col = lambda a, bit: lax.ppermute(a, 'col', xor_pairs(cols, bit))]
    ppermute x16 -> x11, starting transfers between devices: 22.7 us -> 16.2 us  [inner(): swap_col = lambda a, bit: lax.ppermute(a, 'col', xor_pairs(cols, bit))]
    select_n x2 -> x1, other arithmetic: 2.29 us -> 0.09 us  [inner(): lax.select_n(side ^ i, straight[j], second)]
  transfers between devices with their start and end apart: 38 -> 33, of which waited for: 16 -> 17; matrix products, arithmetic and copies ran while one was open for 6% -> 6% of each run, Pallas kernels for 31% -> 21%
where the time goes in v1:
time: 180 us
  waiting for transfers between devices  80.5 us (45%)
  Pallas kernels  58.2 us (32%)
  starting transfers between devices  25.9 us (14%)
  other arithmetic  10.3 us (6%)
  local copies, waits for them, and re-layouts  2.69 us (1%)
    ppermute x22, waiting for transfers between devices, inner(): swap_rep = lambda a, bit: lax.ppermute(a, 'rep', xor_pairs(reps, bit))  64.8 us
    pallas_call x3, Pallas kernels, adam_chunk(): pl.pallas_call(functools.partial(adam_kernel, lanes, bool(chain), previou...  44.6 us
    ppermute x11, starting transfers between devices, inner(): swap_col = lambda a, bit: lax.ppermute(a, 'col', xor_pairs(cols, bit))  16.2 us
    ppermute x11, waiting for transfers between devices, inner(): swap_col = lambda a, bit: lax.ppermute(a, 'col', xor_pairs(cols, bit))  15.7 us
    pallas_call x2, Pallas kernels, down_part(): pl.pallas_call(functools.partial(down_kernel, groups, past is not None),...  13.6 us
    ppermute x22, starting transfers between devices, inner(): swap_rep = lambda a, bit: lax.ppermute(a, 'rep', xor_pairs(reps, bit))  9.61 us
  transfers between devices with their start and end apart: 33, of which 17 were waited for; matrix products, arithmetic and copies ran while one was open for 6% of the time, Pallas kernels for 21%

profile of v1, /device:TPU:0, one launch (start us, length us, event | category | flops | bytes accessed | tf_op | source)
XLA Modules:
  0.0 179.7 jit_solution(12781456674151692675)
XLA Ops:
  0.7 1.2 constant_dynamic-slice_fusion.2
  1.8 0.8 select_reduce_fusion.2
  2.6 0.7 select_reduce_fusion.1
  3.6 5.1 %collective-permute-start.10 = (bf16[96,640]{1,0:T(8,128)(2,1)S(1)}, bf16[96,640]{1,0:T(8,128)(2,1)S(1)}, u32[]{:S(2)}, u32[]{:S(2)}) collective-permute-start(bf16[96,640]{1,0:T(8,128)(2,1)S(1)} %convolution_convert_fusion.1), channel_id=1, source_target_pairs={{0,6},{1,7},{2,4},{3,5},{4,2},{5,3},{6,0},{7,1},{8,14},{9,15},{10,... | collective-permute-start | bytes 368648 | tf_op jit(solution)/shard_map/ppermute | solution.py:230
  8.7 0.6 collective-permute-start.9
  9.4 1.6 collective-permute-start.1
  11.0 0.8 convert_reduce_fusion
  11.8 0.7 fusion.7
  12.4 0.8 select_reduce_fusion
  13.2 1.9 %multiply_convert_fusion = (bf16[256,1152]{1,0:T(8,128)(2,1)S(1)}, bf16[256,1152]{1,0:T(8,128)(2,1)S(1)}, bf16[256,1152]{1,0:T(8,128)(2,1)S(1)}) fusion(bf16[256,3456]{1,0:T(8,128)(2,1)} %param.11, f32[256]{0:T(256)S(1)} %select_reduce_fusion), kind=kLoop, calls=%fused_computation | loop fusion | flops 2654208 | bytes 3539968 | tf_op jit(solution)/shard_map/convert_element_type | solution.py:255
  15.1 4.8 %collective-permute-done.1 = bf16[640,256]{1,0:T(8,128)(2,1)S(1)} collective-permute-done((bf16[640,256]{1,0:T(8,128)(2,1)S(1)}, bf16[640,256]{1,0:T(8,128)(2,1)S(1)}, u32[]{:S(2)}, u32[]{:S(2)}) %collective-permute-start.1) | collective-permute-done | bytes 327712 | tf_op jit(solution)/shard_map/ppermute | solution.py:229
  19.9 1.7 collective-permute-start.2
  21.6 2.7 %collective-permute-done.3 = bf16[640,256]{1,0:T(8,128)(2,1)S(1)} collective-permute-done((bf16[640,256]{1,0:T(8,128)(2,1)S(1)}, bf16[640,256]{1,0:T(8,128)(2,1)S(1)}, u32[]{:S(2)}, u32[]{:S(2)}) %collective-permute-start.3) | collective-permute-done | bytes 327712 | tf_op jit(solution)/shard_map/ppermute | solution.py:229
  24.3 1.5 collective-permute-start.4
  25.8 1.1 select_select_fusion.3
  26.9 0.7 collective-permute-start.11
  27.6 1.4 collective-permute-start.12
  29.1 1.4 constant_dynamic-slice_fusion
  30.5 2.6 %collective-permute-done.11 = bf16[96,640]{1,0:T(8,128)(2,1)S(1)} collective-permute-done((bf16[96,640]{1,0:T(8,128)(2,1)S(1)}, bf16[96,640]{1,0:T(8,128)(2,1)S(1)}, u32[]{:S(2)}, u32[]{:S(2)}) %collective-permute-start.11) | collective-permute-done | bytes 122912 | tf_op jit(solution)/shard_map/ppermute | solution.py:229
  33.1 1.2 collective-permute-start.18
  34.3 1.2 collective-permute-done.13
  35.6 0.9 collective-permute-start.16
  37.2 12.1 %collective-permute-done.19.refs_6_ = bf16[256,1152]{1,0:T(8,128)(2,1)S(1)} collective-permute-done((bf16[256,1152]{1,0:T(8,128)(2,1)S(1)}, bf16[256,1152]{1,0:T(8,128)(2,1)S(1)}, u32[]{:S(2)}, u32[]{:S(2)}) %collective-permute-start.19) | collective-permute-done | bytes 589856 | tf_op jit(solution)/shard_map/ppermute | solution.py:229
  49.7 12.3 %collective-permute-done.16.refs_6_ = bf16[256,1152]{1,0:T(8,128)(2,1)S(1)} collective-permute-done((bf16[256,1152]{1,0:T(8,128)(2,1)S(1)}, bf16[256,1152]{1,0:T(8,128)(2,1)S(1)}, u32[]{:S(2)}, u32[]{:S(2)}) %collective-permute-start.16) | collective-permute-done | bytes 589856 | tf_op jit(solution)/shard_map/ppermute | solution.py:229
  62.8 10.8 %collective-permute-done.6.refs_6_ = bf16[256,1152]{1,0:T(8,128)(2,1)S(1)} collective-permute-done((bf16[256,1152]{1,0:T(8,128)(2,1)S(1)}, bf16[256,1152]{1,0:T(8,128)(2,1)S(1)}, u32[]{:S(2)}, u32[]{:S(2)}) %collective-permute-start.6) | collective-permute-done | bytes 589856 | tf_op jit(solution)/shard_map/ppermute | solution.py:229
  74.1 15.8 %shard_map.129 = (bf16[1280,3456]{1,0:T(8,128)(2,1)}, f32[1280,3456]{1,0:T(8,128)}, f32[1280,3456]{1,0:T(8,128)}) custom-call(bf16[1280,256]{1,0:T(8,128)(2,1)S(1)} %bitcast.26, bf16[1280,256]{1,0:T(8,128)(2,1)S(1)} %collective-permute-done.refs_1_, bf16[1280,256]{1,0:T(8,128)(2,1)S(1)} %pad_maximum_fusion.1.refs_2_, ...), custom_call_target="tpu_custom_call" | custom-call | flops 3019898880 | bytes 29491200 | tf_op jit(solution)/shard_map/pallas_call | solution.py:116
  89.8 14.3 %shard_map.130 = (bf16[1280,3456]{1,0:T(8,128)(2,1)}, f32[1280,3456]{1,0:T(8,128)}, f32[1280,3456]{1,0:T(8,128)}, bf16[2,192,1152]{2,1,0:T(8,128)(2,1)S(1)}, bf16[2,192,1152]{2,1,0:T(8,128)(2,1)S(1)}) custom-call(bf16[1280,256]{1,0:T(8,128)(2,1)S(1)} %bitcast.27, ...), custom_call_target="tpu_custom_call", output_to_operand_aliasing={{0}: (12, {}), {1}: (13, {}), {2}: (14, {})} | custom-call | flops 5284823040 | bytes 29491200 | tf_op jit(solution)/shard_map/pallas_call | solution.py:116
  104.2 14.5 %shard_map.131 = (bf16[1280,3456]{1,0:T(8,128)(2,1)}, f32[1280,3456]{1,0:T(8,128)}, f32[1280,3456]{1,0:T(8,128)}, bf16[1,192,1152]{2,1,0:T(8,128)(2,1)S(1)}, bf16[1,192,1152]{2,1,0:T(8,128)(2,1)S(1)}) custom-call(bf16[1280,256]{1,0:T(8,128)(2,1)S(1)} %bitcast.28, ...), custom_call_target="tpu_custom_call", output_to_operand_aliasing={{0}: (12, {}), {1}: (13, {}), {2}: (14, {})} | custom-call | flops 4152360960 | bytes 29491200 | tf_op jit(solution)/shard_map/pallas_call | solution.py:116
  119.3 1.2 collective-permute-done.21
  120.5 0.7 collective-permute-start.22
  121.2 0.7 collective-permute-done.24
  121.9 1.1 add_convert_fusion
  123.0 0.8 collective-permute-start.25
  123.8 5.1 %collective-permute-done.22 = bf16[1,96,1152]{2,1,0:T(8,128)(2,1)S(1)} collective-permute-done((bf16[1,96,1152]{2,1,0:T(8,128)(2,1)S(1)}, bf16[1,96,1152]{2,1,0:T(8,128)(2,1)S(1)}, u32[]{:S(2)}, u32[]{:S(2)}) %collective-permute-start.22) | collective-permute-done | bytes 221216 | tf_op jit(solution)/shard_map/ppermute | solution.py:229
  129.1 8.4 %collective-permute-done.25 = bf16[2,96,1152]{2,1,0:T(8,128)(2,1)S(1)} collective-permute-done((bf16[2,96,1152]{2,1,0:T(8,128)(2,1)S(1)}, bf16[2,96,1152]{2,1,0:T(8,128)(2,1)S(1)}, u32[]{:S(2)}, u32[]{:S(2)}) %collective-permute-start.25) | collective-permute-done | bytes 442400 | tf_op jit(solution)/shard_map/ppermute | solution.py:229
  137.6 1.3 multiply_convert_fusion.3
  139.0 1.7 collective-permute-done.26
  140.8 8.0 %shard_map.132.refs_5_ = f32[192,2560]{1,0:T(8,128)S(1)} custom-call(s32[2]{0:T(128)S(1)} %pad_add_fusion.refs_0_, bf16[96,1152]{1,0:T(8,128)(2,1)S(1)} %get-tuple-element.66.refs_1_, bf16[96,1152]{1,0:T(8,128)(2,1)S(1)} %get-tuple-element.65.refs_2_, bf16[96,1152]{1,0:T(8,128)(2,1)S(1)} %get-tuple-element.64.refs_3_, ...), custom_call_target="tpu_custom_call" | custom-call | flops 2264924160 | bytes 11796480 | tf_op jit(solution)/shard_map/pallas_call | solution.py:189
  148.8 5.7 %shard_map.133 = (bf16[96,2560]{1,0:T(8,128)(2,1)S(1)}, bf16[96,2560]{1,0:T(8,128)(2,1)S(1)}) custom-call(s32[2]{0:T(128)S(1)} %pad_add_fusion.refs_0_, bf16[96,1152]{1,0:T(8,128)(2,1)S(1)} %fusion.refs_1_, bf16[96,1152]{1,0:T(8,128)(2,1)S(1)} %collective-permute-done.23.refs_2_, bf16[5120,3456]{1,0:T(8,128)(2,1)} %refs_4_.1, bf16[5120,3456]{1,0:T(8,128)(2,1)} %refs_4_.1, ...), custom_call_target="tpu_custom_call" | custom-call | flops 1132462080 | bytes 5898240 | tf_op jit(solution)/shard_map/pallas_call | solution.py:189
  155.1 1.4 collective-permute-start.29
  156.5 6.0 %collective-permute-done.27 = bf16[96,1280]{1,0:T(8,128)(2,1)S(1)} collective-permute-done((bf16[96,1280]{1,0:T(8,128)(2,1)S(1)}, bf16[96,1280]{1,0:T(8,128)(2,1)S(1)}, u32[]{:S(2)}, u32[]{:S(2)}) %collective-permute-start.27) | collective-permute-done | bytes 245792 | tf_op jit(solution)/shard_map/ppermute | solution.py:230
  162.6 1.5 collective-permute-start.28
  164.7 2.8 %collective-permute-done.28 = bf16[96,640]{1,0:T(8,128)(2,1)S(1)} collective-permute-done((bf16[96,640]{1,0:T(8,128)(2,1)S(1)}, bf16[96,640]{1,0:T(8,128)(2,1)S(1)}, u32[]{:S(2)}, u32[]{:S(2)}) %collective-permute-start.28) | collective-permute-done | bytes 122912 | tf_op jit(solution)/shard_map/ppermute | solution.py:230
  167.6 1.5 collective-permute-done.30
  169.3 2.7 %collective-permute-start.31 = (bf16[192,320]{1,0:T(8,128)(2,1)S(1)}, bf16[192,320]{1,0:T(8,128)(2,1)S(1)}, u32[]{:S(2)}, u32[]{:S(2)}) collective-permute-start(bf16[192,320]{1,0:T(8,128)(2,1)S(1)} %pad_maximum_fusion.4), channel_id=1, source_target_pairs={{0,4},{1,5},{2,6},{3,7},{4,0},{5,1},{6,2},{7,3},{8,12},{9,13},{10,... | collective-permute-start | bytes 368648 | tf_op jit(solution)/shard_map/ppermute | solution.py:230
  172.0 5.3 %collective-permute-done.31 = bf16[192,320]{1,0:T(8,128)(2,1)S(1)} collective-permute-done((bf16[192,320]{1,0:T(8,128)(2,1)S(1)}, bf16[192,320]{1,0:T(8,128)(2,1)S(1)}, u32[]{:S(2)}, u32[]{:S(2)}) %collective-permute-start.31) | collective-permute-done | bytes 122912 | tf_op jit(solution)/shard_map/ppermute | solution.py:230
  177.4 1.2 collective-permute-done.32
  178.7 1.0 convolution_convert_fusion
  (70 shorter events, 5.5 us)
Async XLA Ops:
  0.6 2.7 %copy-start = (bf16[128,640]{1,0:T(8,128)(2,1)S(1)}, bf16[128,640]{1,0:T(8,128)(2,1)}, u32[]{:S(2)}) copy-start(bf16[128,640]{1,0:T(8,128)(2,1)} %param.17) | copy-start | bytes 491524
  3.4 6.0 %copy-start.2 = (s32[128]{0:T(128)}, s32[128]{0:T(128)S(1)}, u32[]{:S(2)}) copy-start(s32[128]{0:T(128)S(1)} %compare_select_fusion) | copy-start | bytes 1540
  3.6 22.2 %collective-permute-start.10 = (bf16[96,640]{1,0:T(8,128)(2,1)S(1)}, bf16[96,640]{1,0:T(8,128)(2,1)S(1)}, u32[]{:S(2)}, u32[]{:S(2)}) collective-permute-start(bf16[96,640]{1,0:T(8,128)(2,1)S(1)} %convolution_convert_fusion.1), channel_id=1, source_target_pairs={{0,6},{1,7},{2,4},{3,5},{4,2},{5,3},{6,0},{7,1},{8,14},{9,15},{10,... | collective-permute-start | bytes 368648 | tf_op jit(solution)/shard_map/ppermute | solution.py:230
  8.7 17.1 %collective-permute-start.8 = (bf16[96,640]{1,0:T(8,128)(2,1)S(1)}, bf16[96,640]{1,0:T(8,128)(2,1)}, u32[]{:S(2)}, u32[]{:S(2)}) collective-permute-start(bf16[96,640]{1,0:T(8,128)(2,1)S(1)} %convolution_convert_fusion.1), channel_id=1, source_target_pairs={{0,2},{1,3},{2,0},{3,1},{4,6},{5,7},{6,4},{7,5},{8,10},{9,11},{10,... | collective-permute-start | bytes 368648 | tf_op jit(solution)/shard_map/ppermute | solution.py:230
  8.7 17.1 %collective-permute-start.9 = (bf16[96,640]{1,0:T(8,128)(2,1)S(1)}, bf16[96,640]{1,0:T(8,128)(2,1)}, u32[]{:S(2)}, u32[]{:S(2)}) collective-permute-start(bf16[96,640]{1,0:T(8,128)(2,1)S(1)} %convolution_convert_fusion.1), channel_id=1, source_target_pairs={{0,4},{1,5},{2,6},{3,7},{4,0},{5,1},{6,2},{7,3},{8,12},{9,13},{10,... | collective-permute-start | bytes 368648 | tf_op jit(solution)/shard_map/ppermute | solution.py:230
  9.4 10.6 %collective-permute-start.1 = (bf16[640,256]{1,0:T(8,128)(2,1)S(1)}, bf16[640,256]{1,0:T(8,128)(2,1)S(1)}, u32[]{:S(2)}, u32[]{:S(2)}) collective-permute-start(bf16[640,256]{1,0:T(8,128)(2,1)S(1)} %bitcast.33), channel_id=1, source_target_pairs={{0,16},{8,24},{16,0},{24,8},{1,17},{9,25},{17,1},{25,9},{2,18},{10... | collective-permute-start | bytes 983048 | tf_op jit(solution)/shard_map/ppermute | solution.py:229
  11.0 13.3 %collective-permute-start.3 = (bf16[640,256]{1,0:T(8,128)(2,1)S(1)}, bf16[640,256]{1,0:T(8,128)(2,1)S(1)}, u32[]{:S(2)}, u32[]{:S(2)}) collective-permute-start(bf16[640,256]{1,0:T(8,128)(2,1)S(1)} %bitcast.32), channel_id=1, source_target_pairs={{0,24},{8,16},{16,8},{24,0},{1,25},{9,17},{17,9},{25,1},{2,26},{10... | collective-permute-start | bytes 983048 | tf_op jit(solution)/shard_map/ppermute | solution.py:229
  19.9 15.7 %collective-permute-start.2 = (bf16[640,256]{1,0:T(8,128)(2,1)S(1)}, bf16[640,256]{1,0:T(8,128)(2,1)S(1)}, u32[]{:S(2)}, u32[]{:S(2)}) collective-permute-start(bf16[640,256]{1,0:T(8,128)(2,1)S(1)} %collective-permute-done.1), channel_id=1, source_target_pairs={{0,1},{1,0},{2,3},{3,2},{4,5},{5,4},{6,7},{7,6},{8,9},{9,8},{10,11... | collective-permute-start | bytes 983048 | tf_op jit(solution)/shard_map/ppermute | solution.py:230
  24.3 12.3 %collective-permute-start.4 = (bf16[640,256]{1,0:T(8,128)(2,1)S(1)}, bf16[640,256]{1,0:T(8,128)(2,1)S(1)}, u32[]{:S(2)}, u32[]{:S(2)}) collective-permute-start(bf16[640,256]{1,0:T(8,128)(2,1)S(1)} %collective-permute-done.3), channel_id=1, source_target_pairs={{0,1},{1,0},{2,3},{3,2},{4,5},{5,4},{6,7},{7,6},{8,9},{9,8},{10,11... | collective-permute-start | bytes 983048 | tf_op jit(solution)/shard_map/ppermute | solution.py:230
  26.9 6.3 %collective-permute-start.11 = (bf16[96,640]{1,0:T(8,128)(2,1)S(1)}, bf16[96,640]{1,0:T(8,128)(2,1)S(1)}, u32[]{:S(2)}, u32[]{:S(2)}) collective-permute-start(bf16[96,640]{1,0:T(8,128)(2,1)S(1)} %get-tuple-element.62), channel_id=1, source_target_pairs={{0,16},{8,24},{16,0},{24,8},{1,17},{9,25},{17,1},{25,9},{2,18},{10... | collective-permute-start | bytes 368648 | tf_op jit(solution)/shard_map/ppermute | solution.py:229
  27.6 5.6 %collective-permute-start.12 = (bf16[96,640]{1,0:T(8,128)(2,1)S(1)}, bf16[96,640]{1,0:T(8,128)(2,1)S(1)}, u32[]{:S(2)}, u32[]{:S(2)}) collective-permute-start(bf16[96,640]{1,0:T(8,128)(2,1)S(1)} %get-tuple-element.61), channel_id=1, source_target_pairs={{0,8},{8,0},{16,24},{24,16},{1,9},{9,1},{17,25},{25,17},{2,10},{10... | collective-permute-start | bytes 368648 | tf_op jit(solution)/shard_map/ppermute | solution.py:229
  29.0 6.5 %collective-permute-start.13 = (bf16[96,640]{1,0:T(8,128)(2,1)S(1)}, bf16[96,640]{1,0:T(8,128)(2,1)S(1)}, u32[]{:S(2)}, u32[]{:S(2)}) collective-permute-start(bf16[96,640]{1,0:T(8,128)(2,1)S(1)} %get-tuple-element.60), channel_id=1, source_target_pairs={{0,24},{8,16},{16,8},{24,0},{1,25},{9,17},{17,9},{25,1},{2,26},{10... | collective-permute-start | bytes 368648 | tf_op jit(solution)/shard_map/ppermute | solution.py:229
  33.1 16.2 %collective-permute-start.19 = (bf16[256,1152]{1,0:T(8,128)(2,1)S(1)}, bf16[256,1152]{1,0:T(8,128)(2,1)S(1)}, u32[]{:S(2)}, u32[]{:S(2)}) collective-permute-start(bf16[256,1152]{1,0:T(8,128)(2,1)S(1)} %get-tuple-element.50.refs_4_), channel_id=1, source_target_pairs={{0,16},{8,24},{16,0},{24,8},{1,17},{9,25},{17,1},{25,9},{2,18},{10... | collective-permute-start | bytes 1769480 | tf_op jit(solution)/shard_map/ppermute | solution.py:229
  33.1 16.2 %collective-permute-start.18 = (bf16[256,1152]{1,0:T(8,128)(2,1)S(1)}, bf16[256,1152]{1,0:T(8,128)(2,1)S(1)}, u32[]{:S(2)}, u32[]{:S(2)}) collective-permute-start(bf16[256,1152]{1,0:T(8,128)(2,1)S(1)} %get-tuple-element.50.refs_4_), channel_id=1, source_target_pairs={{0,8},{8,0},{16,24},{24,16},{1,9},{9,1},{17,25},{25,17},{2,10},{10... | collective-permute-start | bytes 1769480 | tf_op jit(solution)/shard_map/ppermute | solution.py:229
  35.5 38.1 %collective-permute-start = (bf16[1280,256]{1,0:T(8,128)(2,1)S(1)}, bf16[1280,256]{1,0:T(8,128)(2,1)S(1)}, u32[]{:S(2)}, u32[]{:S(2)}) collective-permute-start(bf16[1280,256]{1,0:T(8,128)(2,1)S(1)} %bitcast.31), channel_id=1, source_target_pairs={{0,8},{8,0},{16,24},{24,16},{1,9},{9,1},{17,25},{25,17},{2,10},{10... | collective-permute-start | bytes 1966088 | tf_op jit(solution)/shard_map/ppermute | solution.py:229
  35.6 26.3 %collective-permute-start.16 = (bf16[256,1152]{1,0:T(8,128)(2,1)S(1)}, bf16[256,1152]{1,0:T(8,128)(2,1)S(1)}, u32[]{:S(2)}, u32[]{:S(2)}) collective-permute-start(bf16[256,1152]{1,0:T(8,128)(2,1)S(1)} %get-tuple-element.52.refs_4_), channel_id=1, source_target_pairs={{0,16},{8,24},{16,0},{24,8},{1,17},{9,25},{17,1},{25,9},{2,18},{10... | collective-permute-start | bytes 1769480 | tf_op jit(solution)/shard_map/ppermute | solution.py:229
  36.5 25.4 %collective-permute-start.14 = (bf16[384,640]{1,0:T(8,128)(2,1)S(1)}, bf16[384,640]{1,0:T(8,128)(2,1)S(1)}, u32[]{:S(2)}, u32[]{:S(2)}) collective-permute-start(bf16[384,640]{1,0:T(8,128)(2,1)S(1)} %pad_maximum_fusion.3), channel_id=1, source_target_pairs={{0,1},{1,0},{2,3},{3,2},{4,5},{5,4},{6,7},{7,6},{8,9},{9,8},{10,11... | collective-permute-start | bytes 1474568 | tf_op jit(solution)/shard_map/ppermute | solution.py:230
  49.3 24.2 %collective-permute-start.6 = (bf16[256,1152]{1,0:T(8,128)(2,1)S(1)}, bf16[256,1152]{1,0:T(8,128)(2,1)S(1)}, u32[]{:S(2)}, u32[]{:S(2)}) collective-permute-start(bf16[256,1152]{1,0:T(8,128)(2,1)S(1)} %get-tuple-element.51.refs_4_), channel_id=1, source_target_pairs={{0,16},{8,24},{16,0},{24,8},{1,17},{9,25},{17,1},{25,9},{2,18},{10... | collective-permute-start | bytes 1769480 | tf_op jit(solution)/shard_map/ppermute | solution.py:229
  49.3 24.7 %collective-permute-start.20 = (bf16[256,1152]{1,0:T(8,128)(2,1)S(1)}, bf16[256,1152]{1,0:T(8,128)(2,1)S(1)}, u32[]{:S(2)}, u32[]{:S(2)}) collective-permute-start(bf16[256,1152]{1,0:T(8,128)(2,1)S(1)} %collective-permute-done.19.refs_6_), channel_id=1, source_target_pairs={{0,8},{8,0},{16,24},{24,16},{1,9},{9,1},{17,25},{25,17},{2,10},{10... | collective-permute-start | bytes 1769480 | tf_op jit(solution)/shard_map/ppermute | solution.py:229
  62.0 27.9 %collective-permute-start.15 = (bf16[256,1152]{1,0:T(8,128)(2,1)S(1)}, bf16[256,1152]{1,0:T(8,128)(2,1)S(1)}, u32[]{:S(2)}, u32[]{:S(2)}) collective-permute-start(bf16[256,1152]{1,0:T(8,128)(2,1)S(1)} %get-tuple-element.52.refs_4_), channel_id=1, source_target_pairs={{0,8},{8,0},{16,24},{24,16},{1,9},{9,1},{17,25},{25,17},{2,10},{10... | collective-permute-start | bytes 1769480 | tf_op jit(solution)/shard_map/ppermute | solution.py:229
  62.0 27.9 %collective-permute-start.17 = (bf16[256,1152]{1,0:T(8,128)(2,1)S(1)}, bf16[256,1152]{1,0:T(8,128)(2,1)S(1)}, u32[]{:S(2)}, u32[]{:S(2)}) collective-permute-start(bf16[256,1152]{1,0:T(8,128)(2,1)S(1)} %collective-permute-done.16.refs_6_), channel_id=1, source_target_pairs={{0,8},{8,0},{16,24},{24,16},{1,9},{9,1},{17,25},{25,17},{2,10},{10... | collective-permute-start | bytes 1769480 | tf_op jit(solution)/shard_map/ppermute | solution.py:229
  73.5 30.6 %collective-permute-start.5 = (bf16[256,1152]{1,0:T(8,128)(2,1)S(1)}, bf16[256,1152]{1,0:T(8,128)(2,1)S(1)}, u32[]{:S(2)}, u32[]{:S(2)}) collective-permute-start(bf16[256,1152]{1,0:T(8,128)(2,1)S(1)} %get-tuple-element.51.refs_4_), channel_id=1, source_target_pairs={{0,8},{8,0},{16,24},{24,16},{1,9},{9,1},{17,25},{25,17},{2,10},{10... | collective-permute-start | bytes 1769480 | tf_op jit(solution)/shard_map/ppermute | solution.py:229
  73.5 30.6 %collective-permute-start.7 = (bf16[256,1152]{1,0:T(8,128)(2,1)S(1)}, bf16[256,1152]{1,0:T(8,128)(2,1)S(1)}, u32[]{:S(2)}, u32[]{:S(2)}) collective-permute-start(bf16[256,1152]{1,0:T(8,128)(2,1)S(1)} %collective-permute-done.6.refs_6_), channel_id=1, source_target_pairs={{0,8},{8,0},{16,24},{24,16},{1,9},{9,1},{17,25},{25,17},{2,10},{10... | collective-permute-start | bytes 1769480 | tf_op jit(solution)/shard_map/ppermute | solution.py:229
  118.7 1.8 collective-permute-start.21
  118.7 3.2 %collective-permute-start.24 = (bf16[2,192,1152]{2,1,0:T(8,128)(2,1)S(1)}, bf16[2,192,1152]{2,1,0:T(8,128)(2,1)}, u32[]{:S(2)}, u32[]{:S(2)}) collective-permute-start(bf16[2,192,1152]{2,1,0:T(8,128)(2,1)S(1)} %get-tuple-element.41), channel_id=1, source_target_pairs={{0,8},{8,0},{16,24},{24,16},{1,9},{9,1},{17,25},{25,17},{2,10},{10... | collective-permute-start | bytes 2654216 | tf_op jit(solution)/shard_map/ppermute | solution.py:229
  120.5 8.4 %collective-permute-start.22 = (bf16[1,96,1152]{2,1,0:T(8,128)(2,1)S(1)}, bf16[1,96,1152]{2,1,0:T(8,128)(2,1)S(1)}, u32[]{:S(2)}, u32[]{:S(2)}) collective-permute-start(bf16[1,96,1152]{2,1,0:T(8,128)(2,1)S(1)} %add_convert_fusion.3), channel_id=1, source_target_pairs={{0,16},{8,24},{16,0},{24,8},{1,17},{9,25},{17,1},{25,9},{2,18},{10... | collective-permute-start | bytes 663560 | tf_op jit(solution)/shard_map/ppermute | solution.py:229
  123.0 14.6 %collective-permute-start.25 = (bf16[2,96,1152]{2,1,0:T(8,128)(2,1)S(1)}, bf16[2,96,1152]{2,1,0:T(8,128)(2,1)S(1)}, u32[]{:S(2)}, u32[]{:S(2)}) collective-permute-start(bf16[2,96,1152]{2,1,0:T(8,128)(2,1)S(1)} %add_convert_fusion), channel_id=1, source_target_pairs={{0,16},{8,24},{16,0},{24,8},{1,17},{9,25},{17,1},{25,9},{2,18},{10... | collective-permute-start | bytes 1327112 | tf_op jit(solution)/shard_map/ppermute | solution.py:229
  129.1 19.7 %collective-permute-start.23 = (bf16[96,1152]{1,0:T(8,128)(2,1)S(1)}, bf16[96,1152]{1,0:T(8,128)(2,1)S(1)}, u32[]{:S(2)}, u32[]{:S(2)}) collective-permute-start(bf16[96,1152]{1,0:T(8,128)(2,1)S(1)} %fusion.refs_1_), channel_id=1, source_target_pairs={{0,8},{8,0},{16,24},{24,16},{1,9},{9,1},{17,25},{25,17},{2,10},{10... | collective-permute-start | bytes 663560 | tf_op jit(solution)/shard_map/ppermute | solution.py:229
  138.9 1.9 %collective-permute-start.26 = (bf16[2,96,1152]{2,1,0:T(8,128)(2,1)S(1)}, bf16[2,96,1152]{2,1,0:T(8,128)(2,1)S(1)}, u32[]{:S(2)}, u32[]{:S(2)}) collective-permute-start(bf16[2,96,1152]{2,1,0:T(8,128)(2,1)S(1)} %multiply_convert_fusion.3), channel_id=1, source_target_pairs={{0,8},{8,0},{16,24},{24,16},{1,9},{9,1},{17,25},{25,17},{2,10},{10... | collective-permute-start | bytes 1327112 | tf_op jit(solution)/shard_map/ppermute | solution.py:229
  154.5 8.1 %collective-permute-start.27 = (bf16[96,1280]{1,0:T(8,128)(2,1)S(1)}, bf16[96,1280]{1,0:T(8,128)(2,1)S(1)}, u32[]{:S(2)}, u32[]{:S(2)}) collective-permute-start(bf16[96,1280]{1,0:T(8,128)(2,1)S(1)} %slice.92), channel_id=1, source_target_pairs={{0,1},{1,0},{2,3},{3,2},{4,5},{5,4},{6,7},{7,6},{8,9},{9,8},{10,11... | collective-permute-start | bytes 737288 | tf_op jit(solution)/shard_map/ppermute | solution.py:230
  155.1 23.7 %copy-start.3 = (s32[128]{0:T(128)S(1)}, s32[128]{0:T(128)}, u32[]{:S(2)}) copy-start(s32[128]{0:T(128)} %copy-done.2) | copy-start | bytes 1540
  155.1 9.0 %collective-permute-start.29 = (bf16[96,1280]{1,0:T(8,128)(2,1)S(1)}, bf16[96,1280]{1,0:T(8,128)(2,1)S(1)}, u32[]{:S(2)}, u32[]{:S(2)}) collective-permute-start(bf16[96,1280]{1,0:T(8,128)(2,1)S(1)} %slice.96), channel_id=1, source_target_pairs={{0,2},{1,3},{2,0},{3,1},{4,6},{5,7},{6,4},{7,5},{8,10},{9,11},{10,... | collective-permute-start | bytes 737288 | tf_op jit(solution)/shard_map/ppermute | solution.py:230
  162.5 17.2 %copy-start.1 = (bf16[128,640]{1,0:T(8,128)(2,1)S(1)}, bf16[128,640]{1,0:T(8,128)(2,1)}, u32[]{:S(2)}) copy-start(bf16[128,640]{1,0:T(8,128)(2,1)} %param.17) | copy-start | bytes 491524
  162.6 4.9 %collective-permute-start.28 = (bf16[96,640]{1,0:T(8,128)(2,1)S(1)}, bf16[96,640]{1,0:T(8,128)(2,1)S(1)}, u32[]{:S(2)}, u32[]{:S(2)}) collective-permute-start(bf16[96,640]{1,0:T(8,128)(2,1)S(1)} %slice.110), channel_id=1, source_target_pairs={{0,2},{1,3},{2,0},{3,1},{4,6},{5,7},{6,4},{7,5},{8,10},{9,11},{10,... | collective-permute-start | bytes 368648 | tf_op jit(solution)/shard_map/ppermute | solution.py:230
  164.2 4.9 %collective-permute-start.30 = (bf16[96,640]{1,0:T(8,128)(2,1)S(1)}, bf16[96,640]{1,0:T(8,128)(2,1)S(1)}, u32[]{:S(2)}, u32[]{:S(2)}) collective-permute-start(bf16[96,640]{1,0:T(8,128)(2,1)S(1)} %slice.112), channel_id=1, source_target_pairs={{0,1},{1,0},{2,3},{3,2},{4,5},{5,4},{6,7},{7,6},{8,9},{9,8},{10,11... | collective-permute-start | bytes 368648 | tf_op jit(solution)/shard_map/ppermute | solution.py:230
  169.3 8.0 %collective-permute-start.31 = (bf16[192,320]{1,0:T(8,128)(2,1)S(1)}, bf16[192,320]{1,0:T(8,128)(2,1)S(1)}, u32[]{:S(2)}, u32[]{:S(2)}) collective-permute-start(bf16[192,320]{1,0:T(8,128)(2,1)S(1)} %pad_maximum_fusion.4), channel_id=1, source_target_pairs={{0,4},{1,5},{2,6},{3,7},{4,0},{5,1},{6,2},{7,3},{8,12},{9,13},{10,... | collective-permute-start | bytes 368648 | tf_op jit(solution)/shard_map/ppermute | solution.py:230
  177.4 1.3 collective-permute-start.32
